TPU v7x, 32 devices: a whole 2x2x4 slice. The times are simulated.
32 devices in a mesh: dp: 4 (over y, x), ctx: 8 (over z, core).
Axes of the slice: x: 2, y: 2, z: 4, core: 2. Of those that a mesh axis runs over, the one named last changes fastest.
Arguments:
- tokens: bfloat16 [4, 1024, 1152], P('dp', 'ctx'), may hold values from -6 to 6
- starts: int32 [4, 4], P('dp'), may hold values from 0 to 768, as said below
- gain_attn: bfloat16 [1152], P('ctx'), may hold values from 0.099609375 to 1.8984375
- gain_mlp: bfloat16 [1152], P('ctx'), may hold values from 0.099609375 to 1.8984375
- w_query: bfloat16 [1152, 1152], P('ctx', 'dp'), may hold values from -0.1875 to 0.1875
- w_key: bfloat16 [1152, 384], P('ctx', 'dp'), may hold values from -0.1875 to 0.1875
- w_value: bfloat16 [1152, 384], P('ctx', 'dp'), may hold values from -0.1875 to 0.1875
- w_out: bfloat16 [1152, 1152], P('ctx', 'dp'), may hold values from -1.5 to 1.5
- w_gate: bfloat16 [1152, 3072], P('ctx', 'dp'), may hold values from -0.1875 to 0.1875
- w_up: bfloat16 [1152, 3072], P('ctx', 'dp'), may hold values from -0.1875 to 0.1875
- w_down: bfloat16 [3072, 1152], P('ctx', 'dp'), may hold values from -0.109375 to 0.109375
- cotangent: bfloat16 [4, 1024, 1152], P('dp', 'ctx'), may hold values from -6 to 6
Outputs:
- output: bfloat16 [4, 1024, 1152], P('dp', 'ctx')
- input_grad: float32 [4, 1024, 1152], P('dp', 'ctx')
- grad_gain_attn: float32 [1152], P('ctx')
- grad_gain_mlp: float32 [1152], P('ctx')
- grad_query: float32 [1152, 1152], P('ctx', 'dp')
- grad_key: float32 [1152, 384], P('ctx', 'dp')
- grad_value: float32 [1152, 384], P('ctx', 'dp')
- grad_out: float32 [1152, 1152], P('ctx', 'dp')
- grad_gate: float32 [1152, 3072], P('ctx', 'dp')
- grad_up: float32 [1152, 3072], P('ctx', 'dp')
- grad_down: float32 [3072, 1152], P('ctx', 'dp')
Inputs may be any that keep to these rules, and one draw needn't show every extreme that they name: 4 pieces in each sequence, in increasing order; the p-th lies wholly within the p-th of 4 equal parts of the sequence; the first sequence's first piece starts at 0 and the last sequence's last piece ends at the sequence's end.
All inputs are finite; a program needn't handle non-finite values.
Results may differ from a plain program's by a relative error of at most 0.02.
Values may be sent and summed in bfloat16 or wider, within the bound.
A program may use at most 256 MiB of HBM per device.

v0:
```python
import jax
import jax.numpy as jnp
from jax import lax
from jax.sharding import PartitionSpec as P

HEAD_SIZE = 64
PIC = 256
PICS = 4


norm_eps = 1e-05


def rotary_embedding(field, token_positions):
    half = field.shape[-1] // 2
    freqs = 10000.0 ** (-jnp.arange(half).astype(jnp.float32) / half)
    angles = token_positions.astype(jnp.float32)[:, None] * freqs[None, :]
    cosine = jnp.cos(angles)[:, None, :]
    sine = jnp.sin(angles)[:, None, :]
    first = field[..., :half]
    second = field[..., half:]
    return jnp.concatenate(
        [first * cosine - second * sine, second * cosine + first * sine], axis=-1
    )


def rotary_back(field, token_positions):
    half = field.shape[-1] // 2
    freqs = 10000.0 ** (-jnp.arange(half).astype(jnp.float32) / half)
    angles = token_positions.astype(jnp.float32)[:, None] * freqs[None, :]
    cosine = jnp.cos(angles)[:, None, :]
    sine = jnp.sin(angles)[:, None, :]
    first = field[..., :half]
    second = field[..., half:]
    return jnp.concatenate(
        [first * cosine + second * sine, second * cosine - first * sine], axis=-1
    )


def piece_ids(token_positions, seq_starts):
    inside = (token_positions[:, None] >= seq_starts[None, :]) & (
        token_positions[:, None] < seq_starts[None, :] + PIC
    )
    labels = jnp.arange(1, PICS + 1)
    return jnp.sum(jnp.where(inside, labels[None, :], 0), axis=1) - 1


def norm_back(inputs, inverse, gain_vec, upstream):
    scaled = gain_vec * upstream
    return inverse * scaled - inputs * inverse**3 * jnp.mean(
        scaled * inputs, axis=-1, keepdims=True
    )


def fetch_weights(gain_attn, gain_mlp, w_query, w_key, w_value, w_out, w_gate, w_up, w_down):
    wide = (
        lax.all_gather(w_query, "dp", axis=1, tiled=True),
        lax.all_gather(w_key, "dp", axis=1, tiled=True),
        lax.all_gather(w_value, "dp", axis=1, tiled=True),
        lax.all_gather(w_out, "dp", axis=1, tiled=True),
        lax.all_gather(w_gate, "dp", axis=1, tiled=True),
        lax.all_gather(w_up, "dp", axis=1, tiled=True),
        lax.all_gather(w_down, "dp", axis=1, tiled=True),
    )
    return (
        lax.all_gather(gain_attn, "ctx", axis=0, tiled=True),
        lax.all_gather(gain_mlp, "ctx", axis=0, tiled=True),
        lax.all_gather(wide[0], "ctx", axis=0, tiled=True),
        lax.all_gather(wide[1], "ctx", axis=0, tiled=True),
        lax.all_gather(wide[2], "ctx", axis=0, tiled=True),
        lax.all_gather(wide[3], "ctx", axis=0, tiled=True),
        lax.all_gather(wide[4], "ctx", axis=0, tiled=True),
        lax.all_gather(wide[5], "ctx", axis=0, tiled=True),
        lax.all_gather(wide[6], "ctx", axis=0, tiled=True),
    )


def gather_keys(key_rot, value_low):
    return (
        lax.all_gather(key_rot, "ctx", axis=0, tiled=True),
        lax.all_gather(value_low, "ctx", axis=0, tiled=True),
    )


def delta_of(grad_rows, attended_rows):
    return jnp.transpose(jnp.sum(grad_rows.astype(jnp.float32) * attended_rows, axis=-1), (1, 2, 0))


def as_rows(stat):
    return jnp.transpose(stat, (2, 0, 1)).reshape(stat.shape[2], -1)


def body(
    tokens,
    starts,
    gain_attn,
    gain_mlp,
    w_query,
    w_key,
    w_value,
    w_out,
    w_gate,
    w_up,
    w_down,
    cotangent,
):
    tok_count = tokens.shape[1]
    length = tok_count * lax.axis_size("ctx")
    span = min(512, length)
    n_blocks = length // span
    query_pos = lax.axis_index("ctx") * tok_count + jnp.arange(tok_count)
    seq_starts = starts[0]
    labels_all = piece_ids(jnp.arange(length), seq_starts)

    def reach_of(token_positions):
        inside = (token_positions[:, None] >= seq_starts[None, :]) & (
            token_positions[:, None] < seq_starts[None, :] + PIC
        )
        return jnp.maximum(
            token_positions[-1], jnp.max(jnp.where(inside, seq_starts[None, :] + PIC - 1, -1))
        )

    gathered = fetch_weights(
        gain_attn, gain_mlp, w_query, w_key, w_value, w_out, w_gate, w_up, w_down
    )
    (
        gain_first,
        gain_second,
        mat_query,
        key_projection,
        value_projection,
        mat_out,
        mat_gate,
        mat_up,
        mat_down,
    ) = gathered
    heads_kv = key_projection.shape[1] // HEAD_SIZE
    group_size = mat_query.shape[1] // key_projection.shape[1]
    score_scale = HEAD_SIZE ** (-0.5)
    gain_one = gain_first.astype(jnp.float32)
    gain_two = gain_second.astype(jnp.float32)
    stream = tokens[0].astype(jnp.float32)
    inv_one = lax.rsqrt(jnp.mean(stream * stream, axis=-1, keepdims=True) + norm_eps)
    attention_normed = (stream * inv_one * gain_one).astype(jnp.bfloat16)
    query_unrotated = jnp.dot(attention_normed, mat_query, preferred_element_type=jnp.float32)
    key_unrotated = jnp.dot(attention_normed, key_projection, preferred_element_type=jnp.float32)
    v_pre = jnp.dot(attention_normed, value_projection, preferred_element_type=jnp.float32)
    query_vectors = (
        rotary_embedding(query_unrotated.reshape(tok_count, -1, HEAD_SIZE), query_pos)
        .astype(jnp.bfloat16)
        .reshape(tok_count, -1)
    )
    key_rot = (
        rotary_embedding(key_unrotated.reshape(tok_count, heads_kv, HEAD_SIZE), query_pos)
        .astype(jnp.bfloat16)
        .reshape(tok_count, -1)
    )
    value_low = v_pre.astype(jnp.bfloat16)
    key_all, value_all = gather_keys(key_rot, value_low)

    def key_block(source, block_index):
        return lax.dynamic_slice_in_dim(source, block_index * span, span, 0).reshape(
            span, heads_kv, HEAD_SIZE
        )

    def scores_at(block_index, key_piece, query_set, row_pos, row_lab):
        first_key = block_index * span
        key_pos = first_key + jnp.arange(span)
        key_lab = lax.dynamic_slice_in_dim(labels_all, first_key, span, 0)
        raw = (
            jnp.einsum("qhgd,khd->hgqk", query_set, key_piece, preferred_element_type=jnp.float32)
            * score_scale
        )
        allowed = (key_pos[None, :] <= row_pos[:, None]) | (
            row_lab[:, None] == key_lab[None, :]
        ) & (row_lab[:, None] >= 0)
        return jnp.where(allowed[None, None], raw, -1e30)

    keys_now = key_all
    values_now = value_all
    rows = query_vectors.shape[0]
    query_set = query_vectors.reshape(rows, heads_kv, group_size, HEAD_SIZE)
    row_lab = piece_ids(query_pos, seq_starts)
    reach = reach_of(query_pos)

    def lse_step(running, block_index):

        def lse_live(pair_now):
            most_now, sum_now = pair_now
            masked = scores_at(
                block_index, key_block(keys_now, block_index), query_set, query_pos, row_lab
            )
            most_new = jnp.maximum(most_now, jnp.max(masked, axis=-1))
            sum_new = sum_now * jnp.exp(most_now - most_new) + jnp.sum(
                jnp.exp(masked - most_new[..., None]), axis=-1
            )
            return (most_new, sum_new)

        return (
            lax.cond(block_index * span <= reach, lse_live, lambda pair_now: pair_now, running),
            None,
        )

    start_pair = (
        jnp.full((heads_kv, group_size, rows), -1e30, jnp.float32),
        jnp.zeros((heads_kv, group_size, rows), jnp.float32),
    )
    (most_all, sum_all), _ = lax.scan(lse_step, start_pair, jnp.arange(n_blocks))
    log_norm = most_all + jnp.log(sum_all)

    def out_step(running, block_index):

        def out_live(acc_now):
            masked = scores_at(
                block_index, key_block(keys_now, block_index), query_set, query_pos, row_lab
            )
            chances = jnp.exp(masked - log_norm[..., None]).astype(jnp.bfloat16)
            return acc_now + jnp.einsum(
                "hgqk,khd->qhgd",
                chances,
                key_block(values_now, block_index),
                preferred_element_type=jnp.float32,
            )

        return (
            lax.cond(block_index * span <= reach, out_live, lambda acc_now: acc_now, running),
            None,
        )

    attended_set, _ = lax.scan(
        out_step,
        jnp.zeros((rows, heads_kv, group_size, HEAD_SIZE), jnp.float32),
        jnp.arange(n_blocks),
    )
    att_low = attended_set.reshape(tok_count, -1).astype(jnp.bfloat16)
    resid = stream + jnp.dot(att_low, mat_out, preferred_element_type=jnp.float32)
    inv_two = lax.rsqrt(jnp.mean(resid * resid, axis=-1, keepdims=True) + norm_eps)
    normed_m = (resid * inv_two * gain_two).astype(jnp.bfloat16)
    gate_pre = jnp.dot(normed_m, mat_gate, preferred_element_type=jnp.float32)
    up_pre = jnp.dot(normed_m, mat_up, preferred_element_type=jnp.float32)
    sigma = jax.nn.sigmoid(gate_pre)
    silu_val = gate_pre * sigma
    hidden = (silu_val * up_pre).astype(jnp.bfloat16)
    output = (resid + jnp.dot(hidden, mat_down, preferred_element_type=jnp.float32)).astype(
        jnp.bfloat16
    )
    gathered = fetch_weights(
        gain_attn, gain_mlp, w_query, w_key, w_value, w_out, w_gate, w_up, w_down
    )
    (
        gain_first,
        gain_second,
        mat_query,
        key_projection,
        value_projection,
        mat_out,
        mat_gate,
        mat_up,
        mat_down,
    ) = gathered
    key_all, value_all = gather_keys(key_rot, value_low)
    grad_low = cotangent[0]
    grad_resid = grad_low.astype(jnp.float32)
    grad_down = jnp.einsum("tf,td->fd", hidden, grad_low, preferred_element_type=jnp.float32)
    grad_hidden = jnp.einsum("td,fd->tf", grad_low, mat_down, preferred_element_type=jnp.float32)
    grad_gate_pre = (grad_hidden * up_pre * sigma * (1.0 + gate_pre * (1.0 - sigma))).astype(
        jnp.bfloat16
    )
    grad_up_pre = (grad_hidden * silu_val).astype(jnp.bfloat16)
    grad_gate = jnp.einsum("td,tf->df", normed_m, grad_gate_pre, preferred_element_type=jnp.float32)
    grad_up = jnp.einsum("td,tf->df", normed_m, grad_up_pre, preferred_element_type=jnp.float32)
    grad_nm = jnp.einsum("tf,df->td", grad_gate_pre, mat_gate, preferred_element_type=jnp.float32)
    grad_nm = grad_nm + jnp.einsum(
        "tf,df->td", grad_up_pre, mat_up, preferred_element_type=jnp.float32
    )
    grad_gain_two = jnp.sum(grad_nm * resid * inv_two, axis=0)
    grad_resid = grad_resid + norm_back(resid, inv_two, gain_two, grad_nm)
    grad_branch = grad_resid.astype(jnp.bfloat16)
    grad_wo = jnp.einsum("tq,td->qd", att_low, grad_branch, preferred_element_type=jnp.float32)
    grad_att = jnp.einsum(
        "td,qd->tq", grad_branch, mat_out, preferred_element_type=jnp.float32
    ).astype(jnp.bfloat16)
    delta_all = delta_of(grad_att.reshape(tok_count, heads_kv, group_size, HEAD_SIZE), attended_set)
    back_keys_now = key_all
    back_values_now = value_all
    rows = query_vectors.shape[0]
    back_query_set = query_vectors.reshape(rows, heads_kv, group_size, HEAD_SIZE)
    grad_set = grad_att.reshape(rows, heads_kv, group_size, HEAD_SIZE)
    back_row_lab = piece_ids(query_pos, seq_starts)
    back_reach = reach_of(query_pos)

    def back_step(running, block_index):

        def back_live(dq_acc):
            key_piece = key_block(back_keys_now, block_index)
            value_piece = key_block(back_values_now, block_index)
            masked = scores_at(block_index, key_piece, back_query_set, query_pos, back_row_lab)
            chances = jnp.exp(masked - log_norm[..., None])
            upstream = jnp.einsum(
                "qhgd,khd->hgqk", grad_set, value_piece, preferred_element_type=jnp.float32
            )
            score_grad = (chances * (upstream - delta_all[..., None])).astype(jnp.bfloat16)
            return dq_acc + score_scale * jnp.einsum(
                "hgqk,khd->qhgd", score_grad, key_piece, preferred_element_type=jnp.float32
            )

        return (
            lax.cond(block_index * span <= back_reach, back_live, lambda dq_acc: dq_acc, running),
            None,
        )

    dq_set, _ = lax.scan(
        back_step,
        jnp.zeros((rows, heads_kv, group_size, HEAD_SIZE), jnp.float32),
        jnp.arange(n_blocks),
    )
    dq_low = (
        rotary_back(dq_set.reshape(rows, -1, HEAD_SIZE), query_pos)
        .reshape(rows, -1)
        .astype(jnp.bfloat16)
    )
    norm_rows = as_rows(log_norm)
    delta_rows = as_rows(delta_all)
    norm_seq, delta_seq = (
        lax.all_gather(norm_rows, "ctx", axis=0, tiled=True),
        lax.all_gather(delta_rows, "ctx", axis=0, tiled=True),
    )
    own_keys = key_rot.reshape(tok_count, heads_kv, HEAD_SIZE)
    own_values = value_low.reshape(tok_count, heads_kv, HEAD_SIZE)
    own_lab = piece_ids(query_pos, seq_starts)
    start_pair = (
        jnp.zeros((tok_count, heads_kv, HEAD_SIZE), jnp.float32),
        jnp.zeros((tok_count, heads_kv, HEAD_SIZE), jnp.float32),
    )
    query_piece = lax.all_gather(query_vectors, "ctx", axis=0, tiled=True)
    grad_piece = lax.all_gather(grad_att, "ctx", axis=0, tiled=True)
    rows = query_piece.shape[0]
    block = 512

    def one_block(running, block_index):
        first_row = block_index * block
        row_pos = first_row + jnp.arange(block)

        def one_live(pair_now):
            dk_acc, dv_acc = pair_now
            query_set = lax.dynamic_slice_in_dim(query_piece, first_row, block, 0).reshape(
                block, heads_kv, group_size, HEAD_SIZE
            )
            grad_set = lax.dynamic_slice_in_dim(grad_piece, first_row, block, 0).reshape(
                block, heads_kv, group_size, HEAD_SIZE
            )
            lse_set = jnp.transpose(
                lax.dynamic_slice_in_dim(norm_seq, first_row, block, 0).reshape(
                    block, heads_kv, group_size
                ),
                (1, 2, 0),
            )
            delta_set = jnp.transpose(
                lax.dynamic_slice_in_dim(delta_seq, first_row, block, 0).reshape(
                    block, heads_kv, group_size
                ),
                (1, 2, 0),
            )
            row_lab = piece_ids(row_pos, seq_starts)
            raw = (
                jnp.einsum(
                    "qhgd,khd->hgqk", query_set, own_keys, preferred_element_type=jnp.float32
                )
                * score_scale
            )
            allowed = (query_pos[None, :] <= row_pos[:, None]) | (
                row_lab[:, None] == own_lab[None, :]
            ) & (row_lab[:, None] >= 0)
            masked = jnp.where(allowed[None, None], raw, -1e30)
            chances = jnp.exp(masked - lse_set[..., None])
            upstream = jnp.einsum(
                "qhgd,khd->hgqk", grad_set, own_values, preferred_element_type=jnp.float32
            )
            score_grad = (chances * (upstream - delta_set[..., None])).astype(jnp.bfloat16)
            dk_acc = dk_acc + score_scale * jnp.einsum(
                "hgqk,qhgd->khd", score_grad, query_set, preferred_element_type=jnp.float32
            )
            dv_acc = dv_acc + jnp.einsum(
                "hgqk,qhgd->khd",
                chances.astype(jnp.bfloat16),
                grad_set,
                preferred_element_type=jnp.float32,
            )
            return (dk_acc, dv_acc)

        return (
            lax.cond(
                reach_of(row_pos) >= query_pos[0], one_live, lambda pair_now: pair_now, running
            ),
            None,
        )

    result, _ = lax.scan(one_block, start_pair, jnp.arange(rows // block))
    key_grads, value_grads = result
    dk_low = rotary_back(key_grads, query_pos).reshape(tok_count, -1).astype(jnp.bfloat16)
    dv_low = value_grads.reshape(tok_count, -1).astype(jnp.bfloat16)
    grad_wq = jnp.einsum("td,tq->dq", attention_normed, dq_low, preferred_element_type=jnp.float32)
    grad_wk = jnp.einsum("td,tq->dq", attention_normed, dk_low, preferred_element_type=jnp.float32)
    grad_wv = jnp.einsum("td,tq->dq", attention_normed, dv_low, preferred_element_type=jnp.float32)
    grad_na = jnp.einsum("tq,dq->td", dq_low, mat_query, preferred_element_type=jnp.float32)
    grad_na = grad_na + jnp.einsum(
        "tq,dq->td", dk_low, key_projection, preferred_element_type=jnp.float32
    )
    grad_na = grad_na + jnp.einsum(
        "tq,dq->td", dv_low, value_projection, preferred_element_type=jnp.float32
    )
    grad_gain_one = jnp.sum(grad_na * stream * inv_one, axis=0)
    input_grad = grad_resid + norm_back(stream, inv_one, gain_one, grad_na)
    summed = (
        lax.psum_scatter(
            grad_gain_one.astype(jnp.bfloat16), "ctx", scatter_dimension=0, tiled=True
        ).astype(jnp.float32),
        lax.psum_scatter(
            grad_gain_two.astype(jnp.bfloat16), "ctx", scatter_dimension=0, tiled=True
        ).astype(jnp.float32),
        lax.psum_scatter(
            grad_wq.astype(jnp.bfloat16), "ctx", scatter_dimension=0, tiled=True
        ).astype(jnp.float32),
        lax.psum_scatter(
            grad_wk.astype(jnp.bfloat16), "ctx", scatter_dimension=0, tiled=True
        ).astype(jnp.float32),
        lax.psum_scatter(
            grad_wv.astype(jnp.bfloat16), "ctx", scatter_dimension=0, tiled=True
        ).astype(jnp.float32),
        lax.psum_scatter(
            grad_wo.astype(jnp.bfloat16), "ctx", scatter_dimension=0, tiled=True
        ).astype(jnp.float32),
        lax.psum_scatter(
            grad_gate.astype(jnp.bfloat16), "ctx", scatter_dimension=0, tiled=True
        ).astype(jnp.float32),
        lax.psum_scatter(
            grad_up.astype(jnp.bfloat16), "ctx", scatter_dimension=0, tiled=True
        ).astype(jnp.float32),
        lax.psum_scatter(
            grad_down.astype(jnp.bfloat16), "ctx", scatter_dimension=0, tiled=True
        ).astype(jnp.float32),
    )
    shards = (
        lax.psum_scatter(
            summed[2].astype(jnp.bfloat16), "dp", scatter_dimension=1, tiled=True
        ).astype(jnp.float32),
        lax.psum_scatter(
            summed[3].astype(jnp.bfloat16), "dp", scatter_dimension=1, tiled=True
        ).astype(jnp.float32),
        lax.psum_scatter(
            summed[4].astype(jnp.bfloat16), "dp", scatter_dimension=1, tiled=True
        ).astype(jnp.float32),
        lax.psum_scatter(
            summed[5].astype(jnp.bfloat16), "dp", scatter_dimension=1, tiled=True
        ).astype(jnp.float32),
        lax.psum_scatter(
            summed[6].astype(jnp.bfloat16), "dp", scatter_dimension=1, tiled=True
        ).astype(jnp.float32),
        lax.psum_scatter(
            summed[7].astype(jnp.bfloat16), "dp", scatter_dimension=1, tiled=True
        ).astype(jnp.float32),
        lax.psum_scatter(
            summed[8].astype(jnp.bfloat16), "dp", scatter_dimension=1, tiled=True
        ).astype(jnp.float32),
    )
    gain_sums = lax.psum((summed[0], summed[1]), "dp")
    return (
        output[None],
        input_grad[None],
        gain_sums[0],
        gain_sums[1],
        shards[0],
        shards[1],
        shards[2],
        shards[3],
        shards[4],
        shards[5],
        shards[6],
    )


def solution(mesh):
    return jax.shard_map(
        body,
        mesh=mesh,
        in_specs=(
            P("dp", "ctx", None),
            P("dp", None),
            P("ctx"),
            P("ctx"),
            P("ctx", "dp"),
            P("ctx", "dp"),
            P("ctx", "dp"),
            P("ctx", "dp"),
            P("ctx", "dp"),
            P("ctx", "dp"),
            P("ctx", "dp"),
            P("dp", "ctx", None),
        ),
        out_specs=(
            P("dp", "ctx", None),
            P("dp", "ctx", None),
            P("ctx"),
            P("ctx"),
            P("ctx", "dp"),
            P("ctx", "dp"),
            P("ctx", "dp"),
            P("ctx", "dp"),
            P("ctx", "dp"),
            P("ctx", "dp"),
            P("ctx", "dp"),
        ),
        check_vma=False,
    )
```

profile of v0, /device:TPU:0, one launch (start us, length us, event | category | flops | bytes accessed | tf_op | source)
XLA Modules:
  0.0 994.4 jit_solution(5979035751343514435)
XLA Ops:
  31.8 14.4 %all_gather.94 = bf16[144,3072]{1,0:T(8,128)(2,1)} all-gather(bf16[144,768]{1,0:T(8,128)(2,1)S(1)} %copy-done.41), channel_id=1, replica_groups=mesh['dp'=4,'ctx'=8] {'dp'}, dimensions={1}, use_global_device_ids=true | all-gather | bytes 1105920 | tf_op jit(solution)/shard_map/all_gather | solution.py:61
  46.3 14.0 %all_gather.96 = bf16[144,3072]{1,0:T(8,128)(2,1)} all-gather(bf16[144,768]{1,0:T(8,128)(2,1)S(1)} %copy-done.42), channel_id=1, replica_groups=mesh['dp'=4,'ctx'=8] {'dp'}, dimensions={1}, use_global_device_ids=true | all-gather | bytes 1105920 | tf_op jit(solution)/shard_map/all_gather | solution.py:62
  99.1 20.3 %all_gather.84 = bf16[1152,384]{1,0:T(8,128)(2,1)S(1)} all-gather(bf16[144,384]{1,0:T(8,128)(2,1)S(1)} %bitcast.392), channel_id=1, replica_groups=mesh['dp'=4,'ctx'=8] {'ctx'}, dimensions={0}, use_global_device_ids=true | all-gather | bytes 995328 | tf_op jit(solution)/shard_map/all_gather | solution.py:70
  120.2 19.2 %all_gather.85 = bf16[1024,384]{1,0:T(8,128)(2,1)S(1)} all-gather(bf16[128,384]{1,0:T(8,128)(2,1)S(1)} %convolution_convert_fusion.8), channel_id=1, replica_groups=mesh['dp'=4,'ctx'=8] {'ctx'}, dimensions={0}, use_global_device_ids=true | all-gather | bytes 884736 | tf_op jit(solution)/shard_map/all_gather | solution.py:81
  147.9 22.1 %all_gather.87 = bf16[1152,384]{1,0:T(8,128)(2,1)S(1)} all-gather(bf16[144,384]{1,0:T(8,128)(2,1)S(1)} %bitcast.393), channel_id=1, replica_groups=mesh['dp'=4,'ctx'=8] {'ctx'}, dimensions={0}, use_global_device_ids=true | all-gather | bytes 995328 | tf_op jit(solution)/shard_map/all_gather | solution.py:69
  176.4 15.0 %all_gather.88 = bf16[1024,384]{0,1:T(8,128)(2,1)S(1)} all-gather(bf16[128,384]{0,1:T(8,128)(2,1)S(1)} %bitcast.368), channel_id=1, replica_groups=mesh['dp'=4,'ctx'=8] {'ctx'}, dimensions={0}, use_global_device_ids=true | all-gather | bytes 884736 | tf_op jit(solution)/shard_map/all_gather | solution.py:80
  223.4 29.9 %all-gather.18.cloned.1.call-done = bf16[1152,3072]{1,0:T(8,128)(2,1)} async-done(((bf16[144,3072]{1,0:T(8,128)(2,1)}), bf16[1152,3072]{1,0:T(8,128)(2,1)}) %all-gather.18.cloned.1.call-update) | async-done | bytes 7077904 | tf_op jit(solution)/shard_map/all_gather | solution.py:73
  258.7 65.7 %all-gather.20.cloned.1.call-done = bf16[3072,1152]{0,1:T(8,128)(2,1)} async-done(((bf16[384,1152]{0,1:T(8,128)(2,1)}), bf16[3072,1152]{0,1:T(8,128)(2,1)}) %all-gather.20.cloned.1.call-update) | async-done | bytes 7077904 | tf_op jit(solution)/shard_map/all_gather | solution.py:74
  348.8 14.3 %while.60 = (s32[]{:T(128)}, f32[128,6,3,64]{0,3,2,1:T(8,128)}, s32[2]{0:T(128)}, s32[]{:T(128)}, bf16[1024,384]{0,1:T(8,128)(2,1)S(1)}, /*index=5*/s32[128]{0:T...) while((s32[]{:T(128)}, f32[128,6,3,64]{0,3,2,1:T(8,128)}, ...), condition=%wide.region_20.21_spmd.clone, body=%wide.region_17.20_spmd.clone.sunk | while | flops 460620544 | bytes 14122593 | solution.py:312
  370.8 24.1 %all_gather.101 = f32[1024,18]{0,1:T(8,128)} all-gather(f32[128,18]{0,1:T(8,128)S(1)} %reshape.592), channel_id=1, replica_groups=mesh['dp'=4,'ctx'=8] {'ctx'}, dimensions={0}, use_global_device_ids=true | all-gather | bytes 82944 | tf_op jit(solution)/shard_map/all_gather | solution.py:325
  395.0 15.3 %all_gather.103 = f32[1024,18]{0,1:T(8,128)} all-gather(f32[128,18]{0,1:T(8,128)S(1)} %reshape.594), channel_id=1, replica_groups=mesh['dp'=4,'ctx'=8] {'ctx'}, dimensions={0}, use_global_device_ids=true | all-gather | bytes 82944 | tf_op jit(solution)/shard_map/all_gather | solution.py:326
  416.6 61.8 %while.57 = (s32[]{:T(128)}, f32[128,6,64]{0,2,1:T(8,128)}, f32[128,6,64]{0,2,1:T(8,128)}, s32[2]{0:T(128)}, s32[1,4]{1,0:T(1,128)}, /*index=5*/s32[128]{0:T(128...) while((s32[]{:T(128)}, f32[128,6,64]{0,2,1:T(8,128)}, ...), condition=%wide.region_26.27_spmd, body=%wide.region_21.26_spmd.sunk | while | flops 616207872 | bytes 26182308 | solution.py:398
  423.1 24.5 %conditional.11 = ((f32[128,6,64]{0,2,1:T(8,128)}, f32[128,6,64]{0,2,1:T(8,128)})) conditional(s32[]{:T(128)} %convert_element_type.419, (f32[128,6,64]{0,2,1:T(8,128)}, f32[128,6,64]{0,2,1:T(8,128)}) %tuple.162, (s32[]{:T(128)}, bf16[1024,1152]{0,1:T(8,128)(2,1)}, s32[128]{0:T(128)}, s32[512]{0:T(512)S(1)}, s32[1,4]{1,0:T(1,128)}, ...), branch_computations={%region_23.23_spmd, %region_24.25_spmd} | conditional | flops 616197120 | bytes 26177782 | solution.py:392
  454.1 24.3 %conditional.11 = ((f32[128,6,64]{0,2,1:T(8,128)}, f32[128,6,64]{0,2,1:T(8,128)})) conditional(s32[]{:T(128)} %convert_element_type.419, (f32[128,6,64]{0,2,1:T(8,128)}, f32[128,6,64]{0,2,1:T(8,128)}) %tuple.162, (s32[]{:T(128)}, bf16[1024,1152]{0,1:T(8,128)(2,1)}, s32[128]{0:T(128)}, s32[512]{0:T(512)S(1)}, s32[1,4]{1,0:T(1,128)}, ...), branch_computations={%region_23.23_spmd, %region_24.25_spmd} | conditional | flops 616197120 | bytes 26177782 | solution.py:392
  521.9 30.9 %reduce-scatter.29.cloned.1.call-done = bf16[144,384]{1,0:T(8,128)(2,1)} async-done(((bf16[1152,384]{1,0:T(8,128)(2,1)}), bf16[144,384]{1,0:T(8,128)(2,1)}) %reduce-scatter.29.cloned.1.call-update) | async-done | bytes 110608 | tf_op jit(solution)/shard_map/reduce_scatter | solution.py:427
  554.6 75.9 %reduce-scatter.41.cloned.1.call-done = bf16[384,1152]{1,0:T(8,128)(2,1)} async-done(((bf16[3072,1152]{1,0:T(8,128)(2,1)}), bf16[384,1152]{1,0:T(8,128)(2,1)}) %reduce-scatter.41.cloned.1.call-update) | async-done | bytes 884752 | tf_op jit(solution)/shard_map/reduce_scatter | solution.py:439
  632.8 75.7 %reduce-scatter.33.cloned.1.call-done = bf16[144,3072]{1,0:T(8,128)(2,1)} async-done(((bf16[1152,3072]{1,0:T(8,128)(2,1)}), bf16[144,3072]{1,0:T(8,128)(2,1)}) %reduce-scatter.33.cloned.1.call-update) | async-done | bytes 884752 | tf_op jit(solution)/shard_map/reduce_scatter | solution.py:433
  709.2 77.1 %reduce-scatter.37.cloned.1.call-done = bf16[144,3072]{1,0:T(8,128)(2,1)} async-done(((bf16[1152,3072]{1,0:T(8,128)(2,1)}), bf16[144,3072]{1,0:T(8,128)(2,1)}) %reduce-scatter.37.cloned.1.call-update) | async-done | bytes 884752 | tf_op jit(solution)/shard_map/reduce_scatter | solution.py:436
  822.1 19.0 %reduce-scatter.49.cloned.1.call-done = bf16[288,144]{1,0:T(8,128)(2,1)} async-done(((bf16[1152,144]{1,0:T(8,128)(2,1)}), bf16[288,144]{1,0:T(8,128)(2,1)}) %reduce-scatter.49.cloned.1.call-update) | async-done | bytes 82960
  842.9 25.7 %reduce-scatter.45.cloned.1.call-done = bf16[96,144]{1,0:T(8,128)(2,1)} async-done(((bf16[384,144]{1,0:T(8,128)(2,1)}), bf16[96,144]{1,0:T(8,128)(2,1)}) %reduce-scatter.45.cloned.1.call-update) | async-done | bytes 27664
  870.2 25.9 %reduce-scatter.47.cloned.1.call-done = bf16[96,144]{1,0:T(8,128)(2,1)} async-done(((bf16[384,144]{1,0:T(8,128)(2,1)}), bf16[96,144]{1,0:T(8,128)(2,1)}) %reduce-scatter.47.cloned.1.call-update) | async-done | bytes 27664
  897.7 28.3 %reduce-scatter.51.cloned.1.call-done = bf16[288,384]{1,0:T(8,128)(2,1)} async-done(((bf16[1152,384]{1,0:T(8,128)(2,1)}), bf16[288,384]{1,0:T(8,128)(2,1)}) %reduce-scatter.51.cloned.1.call-update) | async-done | bytes 221200
  928.0 27.7 %reduce-scatter.35.cloned.1.call-done = bf16[144,768]{1,0:T(8,128)(2,1)} async-done(((bf16[144,3072]{1,0:T(8,128)(2,1)}), bf16[144,768]{1,0:T(8,128)(2,1)}) %reduce-scatter.35.cloned.1.call-update) | async-done | bytes 221200 | tf_op jit(solution)/shard_map/reduce_scatter | solution.py:456
  957.4 28.2 %reduce-scatter.39.cloned.1.call-done = bf16[144,768]{1,0:T(8,128)(2,1)} async-done(((bf16[144,3072]{1,0:T(8,128)(2,1)}), bf16[144,768]{1,0:T(8,128)(2,1)}) %reduce-scatter.39.cloned.1.call-update) | async-done | bytes 221200 | tf_op jit(solution)/shard_map/reduce_scatter | solution.py:459
  (365 shorter events, 339.8 us)
Async XLA Ops:
  7.2 184.2 %all-gather.12.cloned.1.call-start = ((), (), s32[]{:S(2)}) async-start(), calls=%async_computation.14 | async-start | bytes 2985984 | tf_op jit(solution)/shard_map/all_gather | solution.py:68
  20.3 194.8 %all-gather.14.cloned.1.call-start = ((), (), s32[]{:S(2)}) async-start(), calls=%async_computation.15 | async-start | bytes 2985984 | tf_op jit(solution)/shard_map/all_gather | solution.py:71
  31.7 186.2 %all-gather.16.cloned.1.call-start = ((), (), s32[]{:S(2)}) async-start(), calls=%async_computation.16 | async-start | bytes 7962624 | tf_op jit(solution)/shard_map/all_gather | solution.py:72
  46.2 93.5 %copy-start.49 = (bf16[144,96]{1,0:T(8,128)(2,1)S(1)}, bf16[144,96]{1,0:T(8,128)(2,1)}, u32[]{:S(2)}) copy-start(bf16[144,96]{1,0:T(8,128)(2,1)} %param.33) | copy-start | bytes 82948
  46.2 207.1 %all-gather.18.cloned.1.call-start = ((), (), s32[]{:S(2)}) async-start(), calls=%async_computation.17 | async-start | bytes 7962624 | tf_op jit(solution)/shard_map/all_gather | solution.py:73
  60.3 264.1 %all-gather.20.cloned.1.call-start = ((), (), s32[]{:S(2)}) async-start(), calls=%async_computation.18 | async-start | bytes 7962624 | tf_op jit(solution)/shard_map/all_gather | solution.py:74
  72.4 337.8 %all-gather.24.cloned.1.call-start = ((), (), s32[]{:S(2)}) async-start(), calls=%async_computation.20 | async-start | bytes 2654208 | tf_op jit(solution)/shard_map/all_gather | solution.py:336
  99.1 97.7 %copy-start.50 = (f32[128]{0:T(128)}, f32[128]{0:T(128)S(1)}, u32[]{:S(2)}) copy-start(f32[128]{0:T(128)S(1)} %get-tuple-element.1024) | copy-start | bytes 1540
  223.4 100.9 %copy-start.28 = (bf16[1,128,1152]{2,1,0:T(8,128)(2,1)S(1)}, bf16[1,128,1152]{2,1,0:T(8,128)(2,1)}, u32[]{:S(2)}) copy-start(bf16[1,128,1152]{2,1,0:T(8,128)(2,1)} %param.39) | copy-start | bytes 884740
  342.8 71.9 %all-gather.22.cloned.1.call-start = ((), (), s32[]{:S(2)}) async-start(), calls=%async_computation.19 | async-start | bytes 2654208 | tf_op jit(solution)/shard_map/all_gather | solution.py:335
  343.7 158.2 %reduce-scatter.25.cloned.1.call-start = ((), (), s32[]{:S(2)}) async-start(), calls=%async_computation.21 | async-start | bytes 2985984 | tf_op jit(solution)/shard_map/reduce_scatter | solution.py:421
  367.6 136.4 %reduce-scatter.31.cloned.1.call-start = ((), (), s32[]{:S(2)}) async-start(), calls=%async_computation.24 | async-start | bytes 2985984 | tf_op jit(solution)/shard_map/reduce_scatter | solution.py:430
  370.0 150.1 %reduce-scatter.27.cloned.1.call-start = ((), (), s32[]{:S(2)}) async-start(), calls=%async_computation.22 | async-start | bytes 995328 | tf_op jit(solution)/shard_map/reduce_scatter | solution.py:424
  481.6 71.3 %reduce-scatter.29.cloned.1.call-start = ((), (), s32[]{:S(2)}) async-start(), calls=%async_computation.23 | async-start | bytes 995328 | tf_op jit(solution)/shard_map/reduce_scatter | solution.py:427
  484.7 145.8 %reduce-scatter.41.cloned.1.call-start = ((), (), s32[]{:S(2)}) async-start(), calls=%async_computation.29 | async-start | bytes 7962624 | tf_op jit(solution)/shard_map/reduce_scatter | solution.py:439
  489.8 218.7 %reduce-scatter.33.cloned.1.call-start = ((), (), s32[]{:S(2)}) async-start(), calls=%async_computation.25 | async-start | bytes 7962624 | tf_op jit(solution)/shard_map/reduce_scatter | solution.py:433
  495.8 290.5 %reduce-scatter.37.cloned.1.call-start = ((), (), s32[]{:S(2)}) async-start(), calls=%async_computation.27 | async-start | bytes 7962624 | tf_op jit(solution)/shard_map/reduce_scatter | solution.py:436
  501.8 318.6 %reduce-scatter.43.cloned.1.call-start = ((), (), s32[]{:S(2)}) async-start(), calls=%async_computation.30 | async-start | bytes 737280
  504.0 337.2 %reduce-scatter.49.cloned.1.call-start = ((), (), s32[]{:S(2)}) async-start(), calls=%async_computation.33 | async-start | bytes 737280
  506.1 362.5 %reduce-scatter.45.cloned.1.call-start = ((), (), s32[]{:S(2)}) async-start(), calls=%async_computation.31 | async-start | bytes 245760
  521.9 374.2 %reduce-scatter.47.cloned.1.call-start = ((), (), s32[]{:S(2)}) async-start(), calls=%async_computation.32 | async-start | bytes 245760
  554.6 371.3 %reduce-scatter.51.cloned.1.call-start = ((), (), s32[]{:S(2)}) async-start(), calls=%async_computation.34 | async-start | bytes 1105920
  632.8 322.9 %reduce-scatter.35.cloned.1.call-start = ((), (), s32[]{:S(2)}) async-start(), calls=%async_computation.26 | async-start | bytes 1105920 | tf_op jit(solution)/shard_map/reduce_scatter | solution.py:456
  708.5 277.1 %reduce-scatter.39.cloned.1.call-start = ((), (), s32[]{:S(2)}) async-start(), calls=%async_computation.28 | async-start | bytes 1105920 | tf_op jit(solution)/shard_map/reduce_scatter | solution.py:459
  (57 other events, 836.1 us)
Sparse Core Ops, SparseCore 0:
  20.4 34.1 all-gather.11
  56.8 33.0 all-gather.13
  91.6 89.4 all-gather.15
  182.6 70.7 all-gather.17
  254.8 69.5 all-gather.19
  342.9 29.9 all-gather.23
  375.1 33.0 all-gather.21
  410.5 36.5 reduce-scatter.24
  449.4 37.1 reduce-scatter.30
  488.7 31.3 reduce-scatter.26
  522.4 30.3 reduce-scatter.28
  555.0 75.4 reduce-scatter.40
  632.8 75.6 reduce-scatter.32
  710.6 75.6 reduce-scatter.36
  789.0 23.8 reduce-scatter.42
  815.6 25.4 reduce-scatter.48
  844.3 24.2 reduce-scatter.44
  871.8 24.2 reduce-scatter.46
  899.0 26.8 reduce-scatter.50
  928.7 26.9 reduce-scatter.34
  958.6 26.9 reduce-scatter.38
where the time goes:
time: 1000 us; the launch traced here: 994 us
  waiting for transfers between devices  524 us (52%)
  blocking collectives  233 us (23%)
  matrix products  109 us (11%)
  local copies, waits for them, and re-layouts  65.8 us (7%)
  other arithmetic  31.4 us (3%)
  between operations  18.1 us (2%)
  loops' own time  12.3 us (1%)
    unnamed x26, waiting for transfers between devices  99.3 us
    reduce_scatter x1, waiting for transfers between devices, body(): lax.psum_scatter(grad_up.astype(jnp.bfloat16), 'ctx', scatter_dimension=0...  77.1 us
    reduce_scatter x1, waiting for transfers between devices, body(): lax.psum_scatter(grad_down.astype(jnp.bfloat16), 'ctx', scatter_dimension...  75.9 us
    reduce_scatter x1, waiting for transfers between devices, body(): lax.psum_scatter(grad_gate.astype(jnp.bfloat16), 'ctx', scatter_dimension...  75.7 us
    all_gather x1, waiting for transfers between devices, fetch_weights(): lax.all_gather(wide[6], 'ctx', axis=0, tiled=True)  65.7 us
    reduce_scatter x1, waiting for transfers between devices, body(): lax.psum_scatter(grad_wv.astype(jnp.bfloat16), 'ctx', scatter_dimension=0...  30.9 us
    all_gather x1, waiting for transfers between devices, fetch_weights(): lax.all_gather(wide[5], 'ctx', axis=0, tiled=True)  29.9 us
    reduce_scatter x1, waiting for transfers between devices, body(): lax.psum_scatter(summed[7].astype(jnp.bfloat16), 'dp', scatter_dimension=...  28.2 us
  transfers between devices with their start and end apart: 21, of which 13 were waited for; matrix products, arithmetic and copies ran while one was open for 18% of the time, Pallas kernels for 0%

commit v1 on v0

--- a/solution.py
+++ b/solution.py
@@ -53,26 +53,20 @@
 
 
 def fetch_weights(gain_attn, gain_mlp, w_query, w_key, w_value, w_out, w_gate, w_up, w_down):
-    wide = (
-        lax.all_gather(w_query, "dp", axis=1, tiled=True),
-        lax.all_gather(w_key, "dp", axis=1, tiled=True),
-        lax.all_gather(w_value, "dp", axis=1, tiled=True),
-        lax.all_gather(w_out, "dp", axis=1, tiled=True),
-        lax.all_gather(w_gate, "dp", axis=1, tiled=True),
-        lax.all_gather(w_up, "dp", axis=1, tiled=True),
-        lax.all_gather(w_down, "dp", axis=1, tiled=True),
-    )
-    return (
-        lax.all_gather(gain_attn, "ctx", axis=0, tiled=True),
-        lax.all_gather(gain_mlp, "ctx", axis=0, tiled=True),
-        lax.all_gather(wide[0], "ctx", axis=0, tiled=True),
-        lax.all_gather(wide[1], "ctx", axis=0, tiled=True),
-        lax.all_gather(wide[2], "ctx", axis=0, tiled=True),
-        lax.all_gather(wide[3], "ctx", axis=0, tiled=True),
-        lax.all_gather(wide[4], "ctx", axis=0, tiled=True),
-        lax.all_gather(wide[5], "ctx", axis=0, tiled=True),
-        lax.all_gather(wide[6], "ctx", axis=0, tiled=True),
-    )
+    packed = jnp.concatenate([w_query, w_key, w_value, w_out], axis=1)
+    gains = lax.all_gather(jnp.stack([gain_attn, gain_mlp]), "ctx", axis=1, tiled=True)
+    packed = lax.all_gather(packed, ("dp", "ctx"), axis=0, tiled=True)
+    packed = packed.reshape(lax.axis_size("dp"), -1, packed.shape[1])
+    gate_up = lax.all_gather(jnp.concatenate([w_gate, w_up], axis=1), "ctx", axis=0, tiled=True)
+    down = lax.all_gather(w_down, "ctx", axis=0, tiled=True)
+    cuts = []
+    first = 0
+    for shard in (w_query, w_key, w_value, w_out):
+        part = packed[:, :, first : first + shard.shape[1]]
+        cuts.append(jnp.transpose(part, (1, 0, 2)).reshape(part.shape[1], -1))
+        first += shard.shape[1]
+    ff = w_gate.shape[1]
+    return (gains[0], gains[1], *cuts, gate_up[:, :ff], gate_up[:, ff:], down)
 
 
 def gather_keys(key_rot, value_low):
@@ -236,43 +230,47 @@
     resid = stream + jnp.dot(att_low, mat_out, preferred_element_type=jnp.float32)
     inv_two = lax.rsqrt(jnp.mean(resid * resid, axis=-1, keepdims=True) + norm_eps)
     normed_m = (resid * inv_two * gain_two).astype(jnp.bfloat16)
-    gate_pre = jnp.dot(normed_m, mat_gate, preferred_element_type=jnp.float32)
-    up_pre = jnp.dot(normed_m, mat_up, preferred_element_type=jnp.float32)
+    width = mat_down.shape[1]
+    group_normed = lax.all_gather(normed_m, "dp", axis=0, tiled=True)
+    grad_low = cotangent[0]
+    group_cot = lax.all_gather(grad_low, "dp", axis=0, tiled=True)
+    cot_cols = lax.dynamic_slice_in_dim(group_cot, lax.axis_index("dp") * width, width, 1)
+    grad_hidden_part = jnp.einsum(
+        "td,fd->tf", cot_cols, mat_down, preferred_element_type=jnp.float32
+    ).astype(jnp.bfloat16)
+    grad_hidden = lax.psum_scatter(
+        grad_hidden_part, "dp", scatter_dimension=1, tiled=True
+    ).astype(jnp.float32)
+    gate_pre = jnp.dot(group_normed, mat_gate, preferred_element_type=jnp.float32)
+    up_pre = jnp.dot(group_normed, mat_up, preferred_element_type=jnp.float32)
     sigma = jax.nn.sigmoid(gate_pre)
     silu_val = gate_pre * sigma
     hidden = (silu_val * up_pre).astype(jnp.bfloat16)
-    output = (resid + jnp.dot(hidden, mat_down, preferred_element_type=jnp.float32)).astype(
-        jnp.bfloat16
-    )
-    gathered = fetch_weights(
-        gain_attn, gain_mlp, w_query, w_key, w_value, w_out, w_gate, w_up, w_down
-    )
-    (
-        gain_first,
-        gain_second,
-        mat_query,
-        key_projection,
-        value_projection,
-        mat_out,
-        mat_gate,
-        mat_up,
-        mat_down,
-    ) = gathered
-    key_all, value_all = gather_keys(key_rot, value_low)
-    grad_low = cotangent[0]
+    hidden_all = lax.all_gather(hidden, "dp", axis=1, tiled=True)
+    down_cols = jnp.dot(hidden_all, mat_down, preferred_element_type=jnp.float32)
+    down_rows = lax.all_to_all(
+        down_cols.astype(jnp.bfloat16), "dp", split_axis=0, concat_axis=1, tiled=True
+    )
+    output = (resid + down_rows.astype(jnp.float32)).astype(jnp.bfloat16)
     grad_resid = grad_low.astype(jnp.float32)
-    grad_down = jnp.einsum("tf,td->fd", hidden, grad_low, preferred_element_type=jnp.float32)
-    grad_hidden = jnp.einsum("td,fd->tf", grad_low, mat_down, preferred_element_type=jnp.float32)
+    grad_down = jnp.einsum("tf,td->fd", hidden_all, cot_cols, preferred_element_type=jnp.float32)
     grad_gate_pre = (grad_hidden * up_pre * sigma * (1.0 + gate_pre * (1.0 - sigma))).astype(
         jnp.bfloat16
     )
     grad_up_pre = (grad_hidden * silu_val).astype(jnp.bfloat16)
-    grad_gate = jnp.einsum("td,tf->df", normed_m, grad_gate_pre, preferred_element_type=jnp.float32)
-    grad_up = jnp.einsum("td,tf->df", normed_m, grad_up_pre, preferred_element_type=jnp.float32)
+    grad_gate = jnp.einsum(
+        "td,tf->df", group_normed, grad_gate_pre, preferred_element_type=jnp.float32
+    )
+    grad_up = jnp.einsum(
+        "td,tf->df", group_normed, grad_up_pre, preferred_element_type=jnp.float32
+    )
     grad_nm = jnp.einsum("tf,df->td", grad_gate_pre, mat_gate, preferred_element_type=jnp.float32)
     grad_nm = grad_nm + jnp.einsum(
         "tf,df->td", grad_up_pre, mat_up, preferred_element_type=jnp.float32
     )
+    grad_nm = lax.psum_scatter(
+        grad_nm.astype(jnp.bfloat16), "dp", scatter_dimension=0, tiled=True
+    ).astype(jnp.float32)
     grad_gain_two = jnp.sum(grad_nm * resid * inv_two, axis=0)
     grad_resid = grad_resid + norm_back(resid, inv_two, gain_two, grad_nm)
     grad_branch = grad_resid.astype(jnp.bfloat16)
@@ -300,16 +298,29 @@
                 "qhgd,khd->hgqk", grad_set, value_piece, preferred_element_type=jnp.float32
             )
             score_grad = (chances * (upstream - delta_all[..., None])).astype(jnp.bfloat16)
-            return dq_acc + score_scale * jnp.einsum(
+            key_grad = score_scale * jnp.einsum(
+                "hgqk,qhgd->khd", score_grad, back_query_set, preferred_element_type=jnp.float32
+            )
+            value_grad = jnp.einsum(
+                "hgqk,qhgd->khd",
+                chances.astype(jnp.bfloat16),
+                grad_set,
+                preferred_element_type=jnp.float32,
+            )
+            dq_new = dq_acc + score_scale * jnp.einsum(
                 "hgqk,khd->qhgd", score_grad, key_piece, preferred_element_type=jnp.float32
             )
-
-        return (
-            lax.cond(block_index * span <= back_reach, back_live, lambda dq_acc: dq_acc, running),
-            None,
-        )
-
-    dq_set, _ = lax.scan(
+            return dq_new, (key_grad.astype(jnp.bfloat16), value_grad.astype(jnp.bfloat16))
+
+        none_grad = jnp.zeros((span, heads_kv, HEAD_SIZE), jnp.bfloat16)
+        return lax.cond(
+            block_index * span <= back_reach,
+            back_live,
+            lambda dq_acc: (dq_acc, (none_grad, none_grad)),
+            running,
+        )
+
+    dq_set, kv_parts = lax.scan(
         back_step,
         jnp.zeros((rows, heads_kv, group_size, HEAD_SIZE), jnp.float32),
         jnp.arange(n_blocks),
@@ -319,84 +330,10 @@
         .reshape(rows, -1)
         .astype(jnp.bfloat16)
     )
-    norm_rows = as_rows(log_norm)
-    delta_rows = as_rows(delta_all)
-    norm_seq, delta_seq = (
-        lax.all_gather(norm_rows, "ctx", axis=0, tiled=True),
-        lax.all_gather(delta_rows, "ctx", axis=0, tiled=True),
-    )
-    own_keys = key_rot.reshape(tok_count, heads_kv, HEAD_SIZE)
-    own_values = value_low.reshape(tok_count, heads_kv, HEAD_SIZE)
-    own_lab = piece_ids(query_pos, seq_starts)
-    start_pair = (
-        jnp.zeros((tok_count, heads_kv, HEAD_SIZE), jnp.float32),
-        jnp.zeros((tok_count, heads_kv, HEAD_SIZE), jnp.float32),
-    )
-    query_piece = lax.all_gather(query_vectors, "ctx", axis=0, tiled=True)
-    grad_piece = lax.all_gather(grad_att, "ctx", axis=0, tiled=True)
-    rows = query_piece.shape[0]
-    block = 512
-
-    def one_block(running, block_index):
-        first_row = block_index * block
-        row_pos = first_row + jnp.arange(block)
-
-        def one_live(pair_now):
-            dk_acc, dv_acc = pair_now
-            query_set = lax.dynamic_slice_in_dim(query_piece, first_row, block, 0).reshape(
-                block, heads_kv, group_size, HEAD_SIZE
-            )
-            grad_set = lax.dynamic_slice_in_dim(grad_piece, first_row, block, 0).reshape(
-                block, heads_kv, group_size, HEAD_SIZE
-            )
-            lse_set = jnp.transpose(
-                lax.dynamic_slice_in_dim(norm_seq, first_row, block, 0).reshape(
-                    block, heads_kv, group_size
-                ),
-                (1, 2, 0),
-            )
-            delta_set = jnp.transpose(
-                lax.dynamic_slice_in_dim(delta_seq, first_row, block, 0).reshape(
-                    block, heads_kv, group_size
-                ),
-                (1, 2, 0),
-            )
-            row_lab = piece_ids(row_pos, seq_starts)
-            raw = (
-                jnp.einsum(
-                    "qhgd,khd->hgqk", query_set, own_keys, preferred_element_type=jnp.float32
-                )
-                * score_scale
-            )
-            allowed = (query_pos[None, :] <= row_pos[:, None]) | (
-                row_lab[:, None] == own_lab[None, :]
-            ) & (row_lab[:, None] >= 0)
-            masked = jnp.where(allowed[None, None], raw, -1e30)
-            chances = jnp.exp(masked - lse_set[..., None])
-            upstream = jnp.einsum(
-                "qhgd,khd->hgqk", grad_set, own_values, preferred_element_type=jnp.float32
-            )
-            score_grad = (chances * (upstream - delta_set[..., None])).astype(jnp.bfloat16)
-            dk_acc = dk_acc + score_scale * jnp.einsum(
-                "hgqk,qhgd->khd", score_grad, query_set, preferred_element_type=jnp.float32
-            )
-            dv_acc = dv_acc + jnp.einsum(
-                "hgqk,qhgd->khd",
-                chances.astype(jnp.bfloat16),
-                grad_set,
-                preferred_element_type=jnp.float32,
-            )
-            return (dk_acc, dv_acc)
-
-        return (
-            lax.cond(
-                reach_of(row_pos) >= query_pos[0], one_live, lambda pair_now: pair_now, running
-            ),
-            None,
-        )
-
-    result, _ = lax.scan(one_block, start_pair, jnp.arange(rows // block))
-    key_grads, value_grads = result
+    kv_parts = jnp.concatenate([part.reshape(length, -1) for part in kv_parts], axis=1)
+    kv_sums = lax.psum_scatter(kv_parts, "ctx", scatter_dimension=0, tiled=True).astype(jnp.float32)
+    key_grads = kv_sums[:, : heads_kv * HEAD_SIZE].reshape(tok_count, heads_kv, HEAD_SIZE)
+    value_grads = kv_sums[:, heads_kv * HEAD_SIZE :]
     dk_low = rotary_back(key_grads, query_pos).reshape(tok_count, -1).astype(jnp.bfloat16)
     dv_low = value_grads.reshape(tok_count, -1).astype(jnp.bfloat16)
     grad_wq = jnp.einsum("td,tq->dq", attention_normed, dq_low, preferred_element_type=jnp.float32)
@@ -411,59 +348,47 @@
     )
     grad_gain_one = jnp.sum(grad_na * stream * inv_one, axis=0)
     input_grad = grad_resid + norm_back(stream, inv_one, gain_one, grad_na)
-    summed = (
-        lax.psum_scatter(
-            grad_gain_one.astype(jnp.bfloat16), "ctx", scatter_dimension=0, tiled=True
-        ).astype(jnp.float32),
-        lax.psum_scatter(
-            grad_gain_two.astype(jnp.bfloat16), "ctx", scatter_dimension=0, tiled=True
-        ).astype(jnp.float32),
-        lax.psum_scatter(
-            grad_wq.astype(jnp.bfloat16), "ctx", scatter_dimension=0, tiled=True
-        ).astype(jnp.float32),
-        lax.psum_scatter(
-            grad_wk.astype(jnp.bfloat16), "ctx", scatter_dimension=0, tiled=True
-        ).astype(jnp.float32),
-        lax.psum_scatter(
-            grad_wv.astype(jnp.bfloat16), "ctx", scatter_dimension=0, tiled=True
-        ).astype(jnp.float32),
-        lax.psum_scatter(
-            grad_wo.astype(jnp.bfloat16), "ctx", scatter_dimension=0, tiled=True
-        ).astype(jnp.float32),
-        lax.psum_scatter(
-            grad_gate.astype(jnp.bfloat16), "ctx", scatter_dimension=0, tiled=True
-        ).astype(jnp.float32),
-        lax.psum_scatter(
-            grad_up.astype(jnp.bfloat16), "ctx", scatter_dimension=0, tiled=True
-        ).astype(jnp.float32),
-        lax.psum_scatter(
-            grad_down.astype(jnp.bfloat16), "ctx", scatter_dimension=0, tiled=True
-        ).astype(jnp.float32),
-    )
+    n_dp = lax.axis_size("dp")
+    n_ctx = lax.axis_size("ctx")
+    cut = jnp.concatenate(
+        [
+            jnp.transpose(
+                part.astype(jnp.bfloat16).reshape(part.shape[0], n_dp, -1), (1, 0, 2)
+            )
+            for part in (grad_wq, grad_wk, grad_wv, grad_wo)
+        ],
+        axis=2,
+    )
+    mine = lax.psum_scatter(
+        cut.reshape(-1, cut.shape[2]), ("dp", "ctx"), scatter_dimension=0, tiled=True
+    ).astype(jnp.float32)
+    gate_up_sum = lax.psum_scatter(
+        jnp.concatenate([grad_gate, grad_up], axis=1).astype(jnp.bfloat16),
+        "ctx",
+        scatter_dimension=0,
+        tiled=True,
+    ).astype(jnp.float32)
+    down_sum = lax.psum_scatter(
+        grad_down.astype(jnp.bfloat16), "ctx", scatter_dimension=0, tiled=True
+    ).astype(jnp.float32)
+    ff = w_gate.shape[1]
+    e_one = w_query.shape[1]
+    e_two = e_one + w_key.shape[1]
+    e_three = e_two + w_value.shape[1]
     shards = (
-        lax.psum_scatter(
-            summed[2].astype(jnp.bfloat16), "dp", scatter_dimension=1, tiled=True
-        ).astype(jnp.float32),
-        lax.psum_scatter(
-            summed[3].astype(jnp.bfloat16), "dp", scatter_dimension=1, tiled=True
-        ).astype(jnp.float32),
-        lax.psum_scatter(
-            summed[4].astype(jnp.bfloat16), "dp", scatter_dimension=1, tiled=True
-        ).astype(jnp.float32),
-        lax.psum_scatter(
-            summed[5].astype(jnp.bfloat16), "dp", scatter_dimension=1, tiled=True
-        ).astype(jnp.float32),
-        lax.psum_scatter(
-            summed[6].astype(jnp.bfloat16), "dp", scatter_dimension=1, tiled=True
-        ).astype(jnp.float32),
-        lax.psum_scatter(
-            summed[7].astype(jnp.bfloat16), "dp", scatter_dimension=1, tiled=True
-        ).astype(jnp.float32),
-        lax.psum_scatter(
-            summed[8].astype(jnp.bfloat16), "dp", scatter_dimension=1, tiled=True
-        ).astype(jnp.float32),
-    )
-    gain_sums = lax.psum((summed[0], summed[1]), "dp")
+        mine[:, :e_one],
+        mine[:, e_one:e_two],
+        mine[:, e_two:e_three],
+        mine[:, e_three:],
+        gate_up_sum[:, :ff],
+        gate_up_sum[:, ff:],
+        down_sum,
+    )
+    gain_both = lax.psum(jnp.stack([grad_gain_one, grad_gain_two]), ("dp", "ctx"))
+    gain_rows = gain_attn.shape[0]
+    gain_sums = lax.dynamic_slice_in_dim(
+        gain_both, lax.axis_index("ctx") * gain_rows, gain_rows, 1
+    )
     return (
         output[None],
         input_grad[None],

time: 1000 us -> 652 us (0.65)
  waiting for transfers between devices: 524 us -> 373 us
  blocking collectives: 233 us -> 90.2 us
  matrix products: 109 us -> 55.7 us
    reduce_scatter x9 -> x3, waiting for transfers between devices: 329 us -> 182 us  [the longest x1 112 us: body(): lax.psum_scatter(cut.reshape(-1, cut.shape[2]), ('dp', 'ctx'), scatter_di...]
    all_gather x11 -> x1, blocking collectives: 160 us -> 13.5 us  [fetch_weights(): lax.all_gather(jnp.stack([gain_attn, gain_mlp]), 'ctx', axis=1, tiled=True)]
    unnamed x26 -> x15, waiting for transfers between devices: 99.3 us -> 38.5 us
    all_gather x7 -> x6, waiting for transfers between devices: 95.6 us -> 147 us  [the longest x1 53.4 us: fetch_weights(): packed = lax.all_gather(packed, ('dp', 'ctx'), axis=0, tiled=True)]
    dot_general x13 -> x10, matrix products: 67.6 us -> 29 us  [the longest x1 5.16 us: body(): jnp.einsum('td,fd->tf', cot_cols, mat_down, preferred_element_type=jnp.fl...]
    psum x1, blocking collectives: 10.5 us -> 38.7 us  [body(): lax.psum(jnp.stack([grad_gain_one, grad_gain_two]), ('dp', 'ctx'))]
    unnamed x2 -> x0, blocking collectives: 27.8 us -> none
    transpose x0 -> x6, local copies, waits for them, and re-layouts: none -> 20.5 us  [fetch_weights(): cuts.append(jnp.transpose(part, (1, 0, 2)).reshape(part.shape[1], -1))]
  transfers between devices with their start and end apart: 21 -> 13, of which waited for: 13 -> 10; matrix products, arithmetic and copies ran while one was open for 18% -> 17% of each run, Pallas kernels for 0% -> 0%
where the time goes in v1:
time: 652 us; the launch traced here: 645 us
  waiting for transfers between devices  373 us (57%)
  blocking collectives  90.2 us (14%)
  local copies, waits for them, and re-layouts  73.2 us (11%)
  matrix products  55.7 us (9%)
  other arithmetic  24.7 us (4%)
  between operations  16.7 us (3%)
    reduce_scatter x1, waiting for transfers between devices, body(): lax.psum_scatter(cut.reshape(-1, cut.shape[2]), ('dp', 'ctx'), scatter_di...  112 us
    all_gather x1, waiting for transfers between devices, fetch_weights(): packed = lax.all_gather(packed, ('dp', 'ctx'), axis=0, tiled=True)  53.4 us
    all_gather x1, waiting for transfers between devices, body(): hidden_all = lax.all_gather(hidden, 'dp', axis=1, tiled=True)  44 us
    reduce_scatter x1, waiting for transfers between devices, body(): lax.psum_scatter(grad_hidden_part, 'dp', scatter_dimension=1, tiled=True)  42.6 us
    psum x1, blocking collectives, body(): lax.psum(jnp.stack([grad_gain_one, grad_gain_two]), ('dp', 'ctx'))  38.7 us
    unnamed x15, waiting for transfers between devices  38.5 us
    all_gather x1, waiting for transfers between devices, body(): group_normed = lax.all_gather(normed_m, 'dp', axis=0, tiled=True)  28.7 us
    reduce_scatter x1, waiting for transfers between devices, body(): lax.psum_scatter(grad_nm.astype(jnp.bfloat16), 'dp', scatter_dimension=0,...  28.1 us
  transfers between devices with their start and end apart: 13, of which 10 were waited for; matrix products, arithmetic and copies ran while one was open for 17% of the time, Pallas kernels for 0%

profile of v1, /device:TPU:0, one launch (start us, length us, event | category | flops | bytes accessed | tf_op | source)
XLA Modules:
  0.0 644.7 jit_solution(1593376494850298752)
XLA Ops:
  14.6 13.5 %all-gather.1 = bf16[8,144,2]{1,2,0:T(2,128)(2,1)S(1)} all-gather(bf16[1,144,2]{1,2,0:T(2,128)(2,1)S(1)} %maximum_bitcast_fusion), channel_id=1, replica_groups=mesh['dp'=4,'ctx'=8] {'ctx'}, dimensions={0}, use_global_device_ids=true | all-gather | bytes 5184 | tf_op jit(solution)/shard_map/all_gather | solution.py:57
  33.0 53.4 %all-gather.9.cloned.1.call-done = bf16[4608,768]{1,0:T(8,128)(2,1)} async-done(((bf16[144,768]{1,0:T(8,128)(2,1)}), bf16[4608,768]{1,0:T(8,128)(2,1)}) %all-gather.9.cloned.1.call-update) | async-done | bytes 7077904 | tf_op jit(solution)/shard_map/all_gather | solution.py:58
  90.3 15.5 %all_gather.29 = bf16[1024,384]{1,0:T(8,128)(2,1)S(1)} all-gather(bf16[128,384]{1,0:T(8,128)(2,1)S(1)} %convolution_convert_fusion.10), channel_id=1, replica_groups=mesh['dp'=4,'ctx'=8] {'ctx'}, dimensions={0}, use_global_device_ids=true | all-gather | bytes 884736 | tf_op jit(solution)/shard_map/all_gather | solution.py:75
  107.4 7.9 %slice_bitcast_fusion = (bf16[1152,4,288]{2,0,1:T(8,128)(2,1)}, bf16[1152,4,288]{2,0,1:T(8,128)(2,1)}) fusion(bf16[4,1152,768]{2,1,0:T(8,128)(2,1)} %bitcast.296), kind=kLoop, calls=%fused_computation.63 | loop fusion | bytes 10616832 | tf_op jit(solution)/shard_map/transpose | solution.py:66
  123.6 22.5 %all_gather.30 = bf16[1024,384]{0,1:T(8,128)(2,1)S(1)} all-gather(bf16[128,384]{0,1:T(8,128)(2,1)S(1)} %bitcast.323), channel_id=1, replica_groups=mesh['dp'=4,'ctx'=8] {'ctx'}, dimensions={0}, use_global_device_ids=true | all-gather | bytes 884736 | tf_op jit(solution)/shard_map/all_gather | solution.py:74
  146.1 5.5 while.45
  151.7 5.2 while.46
  157.0 5.0 copy.116
  165.8 5.2 convolution_convert_fusion.2
  171.1 20.8 %all-gather.13.cloned.1.call-done = bf16[1152,1536]{1,0:T(8,128)(2,1)} async-done(((bf16[144,1536]{1,0:T(8,128)(2,1)}), bf16[1152,1536]{1,0:T(8,128)(2,1)}) %all-gather.13.cloned.1.call-update) | async-done | bytes 3538960 | tf_op jit(solution)/shard_map/all_gather | solution.py:60
  191.9 28.7 %all-gather.11.cloned.1.call-done = bf16[512,1152]{1,0:T(8,128)(2,1)} async-done(((bf16[128,1152]{1,0:T(8,128)(2,1)}), bf16[512,1152]{1,0:T(8,128)(2,1)}) %all-gather.11.cloned.1.call-update) | async-done | bytes 1179664 | tf_op jit(solution)/shard_map/all_gather | solution.py:234
  224.8 42.6 %reduce-scatter.13.cloned.1.call-done = bf16[512,768]{1,0:T(8,128)(2,1)} async-done(((bf16[512,3072]{1,0:T(8,128)(2,1)}), bf16[512,768]{1,0:T(8,128)(2,1)}) %reduce-scatter.13.cloned.1.call-update) | async-done | bytes 786448 | tf_op jit(solution)/shard_map/reduce_scatter | solution.py:241
  267.3 5.1 fusion.50
  278.2 28.1 %reduce-scatter.15.cloned.1.call-done = bf16[128,1152]{1,0:T(8,128)(2,1)} async-done(((bf16[512,1152]{1,0:T(8,128)(2,1)}), bf16[128,1152]{1,0:T(8,128)(2,1)}) %reduce-scatter.15.cloned.1.call-update) | async-done | bytes 294928 | tf_op jit(solution)/shard_map/reduce_scatter | solution.py:271
  308.0 44.0 %all-gather.15.cloned.1.call-done = bf16[512,3072]{1,0:T(8,128)(2,1)} async-done(((bf16[512,768]{1,0:T(8,128)(2,1)}), bf16[512,3072]{1,0:T(8,128)(2,1)}) %all-gather.15.cloned.1.call-update) | async-done | bytes 3145744 | tf_op jit(solution)/shard_map/all_gather | solution.py:249
  359.8 5.6 all-to-all-done
  371.5 10.8 %while.47 = (s32[]{:T(128)}, f32[128,6,3,64]{0,3,2,1:T(8,128)S(1)}, bf16[2,512,6,64]{1,3,2,0:T(8,128)(2,1)}, bf16[2,512,6,64]{1,3,2,0:T(8,128)(2,1)}, s32[2]{0:T...) while((s32[]{:T(128)}, f32[128,6,3,64]{0,3,2,1:T(8,128)S(1)}, ...), condition=%wide.region_22.23_spmd.clone, body=%wide.region_19.22_spmd.clone.sunk | while | flops 767918848 | bytes 30122656 | solution.py:323
  372.8 6.1 conditional.11
  393.8 5.8 copy.139
  409.7 17.8 %reduce-scatter.19.cloned.1.call-done = bf16[128,768]{1,0:T(8,128)(2,1)} async-done(((bf16[1024,768]{1,0:T(8,128)(2,1)}), bf16[128,768]{1,0:T(8,128)(2,1)}) %reduce-scatter.19.cloned.1.call-update) | async-done | bytes 196624
  438.5 10.3 %copy.123 = bf16[4,1152,768]{2,1,0:T(8,128)(2,1)} copy(bf16[4,1152,768]{1,2,0:T(8,128)(2,1)} %pad_maximum_fusion) | data formatting | bytes 14155776 | tf_op jit(solution)/shard_map/concatenate | solution.py:353
  453.0 18.7 %reduce-scatter.21.cloned.1.call-done = bf16[144,1536]{1,0:T(8,128)(2,1)} async-done(((bf16[1152,1536]{1,0:T(8,128)(2,1)}), bf16[144,1536]{1,0:T(8,128)(2,1)}) %reduce-scatter.21.cloned.1.call-update) | async-done | bytes 442384
  480.1 38.7 %psum.7 = f32[2,1152]{1,0:T(2,128)S(1)} all-reduce(f32[2,1152]{1,0:T(2,128)S(1)} %pad_maximum_fusion.9), channel_id=1, replica_groups=mesh['dp'=4,'ctx'=8] {'dp','ctx'}, use_global_device_ids=true, to_apply=%region_27.28 | all-reduce | flops 2304 | bytes 18432 | tf_op jit(solution)/shard_map/psum | solution.py:387
  522.5 111.7 %reduce-scatter.17.cloned.1.call-done = bf16[144,768]{1,0:T(8,128)(2,1)} async-done(((bf16[4608,768]{1,0:T(8,128)(2,1)}), bf16[144,768]{1,0:T(8,128)(2,1)}) %reduce-scatter.17.cloned.1.call-update) | async-done | bytes 221200 | tf_op jit(solution)/shard_map/reduce_scatter | solution.py:362
  (257 shorter events, 126.4 us)
Async XLA Ops:
  7.2 21.6 %copy-start.31 = (s32[1,4]{1,0:T(1,128)S(1)}, s32[1,4]{1,0:T(1,128)}, u32[]{:S(2)}) copy-start(s32[1,4]{1,0:T(1,128)} %param.25) | copy-start | bytes 52
  7.2 24.3 %copy-start.2 = (bf16[1,128,1152]{2,1,0:T(8,128)(2,1)S(1)}, bf16[1,128,1152]{2,1,0:T(8,128)(2,1)}, u32[]{:S(2)}) copy-start(bf16[1,128,1152]{2,1,0:T(8,128)(2,1)} %param.24) | copy-start | bytes 884740
  7.2 79.2 %all-gather.9.cloned.1.call-start = ((), (), s32[]{:S(2)}) async-start(), calls=%async_computation.7 | async-start | bytes 7299072 | tf_op jit(solution)/shard_map/all_gather | solution.py:58
  9.1 156.7 %all-gather.19.cloned.1.call-start = ((), (), s32[]{:S(2)}) async-start(), calls=%async_computation.15 | async-start | bytes 1474560 | tf_op jit(solution)/shard_map/all_gather | solution.py:236
  9.9 156.0 %all-gather.17.cloned.1.call-start = ((), (), s32[]{:S(2)}) async-start(), calls=%async_computation.11 | async-start | bytes 1990656 | tf_op jit(solution)/shard_map/all_gather | solution.py:61
  10.6 181.3 %all-gather.13.cloned.1.call-start = ((), (), s32[]{:S(2)}) async-start(), calls=%async_computation.9 | async-start | bytes 3981312 | tf_op jit(solution)/shard_map/all_gather | solution.py:60
  12.5 208.1 %all-gather.11.cloned.1.call-start = ((), (), s32[]{:S(2)}) async-start(), calls=%async_computation.8 | async-start | bytes 1474560 | tf_op jit(solution)/shard_map/all_gather | solution.py:234
  115.4 6.1 copy-start.21
  115.4 6.1 copy-start.23
  157.0 5.1 copy-start.10
  157.0 5.0 copy-start.14
  157.0 5.0 copy-start.3
  165.7 101.6 %reduce-scatter.13.cloned.1.call-start = ((), (), s32[]{:S(2)}) async-start(), calls=%async_computation.12 | async-start | bytes 3932160 | tf_op jit(solution)/shard_map/reduce_scatter | solution.py:241
  171.0 135.2 %reduce-scatter.15.cloned.1.call-start = ((), (), s32[]{:S(2)}) async-start(), calls=%async_computation.13 | async-start | bytes 1474560 | tf_op jit(solution)/shard_map/reduce_scatter | solution.py:271
  267.3 6.0 copy-start.33
  277.4 74.6 %all-gather.15.cloned.1.call-start = ((), (), s32[]{:S(2)}) async-start(), calls=%async_computation.10 | async-start | bytes 3932160 | tf_op jit(solution)/shard_map/all_gather | solution.py:249
  356.3 9.2 %all-to-all-start = ((bf16[4,128,288]{1,2,0:T(8,128)(2,1)}), bf16[4,128,288]{1,2,0:T(8,128)(2,1)S(1)}, u32[]{:S(2)}, u32[]{:S(2)}) async-start(bf16[4,128,288]{1,2,0:T(8,128)(2,1)} %bitcast.279), calls=%async_computation | async-start | bytes 589824 | tf_op jit(solution)/shard_map/all_to_all | solution.py:251
  359.8 67.8 %reduce-scatter.19.cloned.1.call-start = ((), (), s32[]{:S(2)}) async-start(), calls=%async_computation.16 | async-start | bytes 1769472
  387.2 84.4 %reduce-scatter.21.cloned.1.call-start = ((), (), s32[]{:S(2)}) async-start(), calls=%async_computation.17 | async-start | bytes 3981312
  399.6 120.9 %reduce-scatter.23.cloned.1.call-start = ((), (), s32[]{:S(2)}) async-start(), calls=%async_computation.18 | async-start | bytes 2654208
  405.4 228.8 %reduce-scatter.17.cloned.1.call-start = ((), (), s32[]{:S(2)}) async-start(), calls=%async_computation.14 | async-start | bytes 7299072 | tf_op jit(solution)/shard_map/reduce_scatter | solution.py:362
  474.0 4.7 copy-start.13
  474.0 4.7 copy-start.29
  477.2 42.2 %copy-start.32 = (f32[128]{0:T(128)S(1)}, f32[128]{0:T(128)}, u32[]{:S(2)}) copy-start(f32[128]{0:T(128)} %get-tuple-element.737) | copy-start | bytes 1540
  (29 other events, 68.2 us)
Sparse Core Ops, SparseCore 0:
  11.6 74.7 all-gather.8
  88.3 26.1 all-gather.18
  116.0 32.6 all-gather.16
  150.8 41.0 all-gather.12
  194.1 26.4 all-gather.10
  223.4 43.8 reduce-scatter.12
  277.5 28.6 reduce-scatter.14
  308.1 43.8 all-gather.14
  387.3 40.1 reduce-scatter.18
  429.7 41.9 reduce-scatter.20
  474.0 35.5 reduce-scatter.22
  515.1 118.9 reduce-scatter.16

commit v2 on v1

--- a/solution.py
+++ b/solution.py
@@ -1,6 +1,10 @@
+import functools
+
 import jax
 import jax.numpy as jnp
 from jax import lax
+from jax.experimental import pallas as pl
+from jax.experimental.pallas import tpu as pltpu
 from jax.sharding import PartitionSpec as P
 
 HEAD_SIZE = 64
@@ -404,9 +408,890 @@
     )
 
 
+BF = jnp.bfloat16
+F32 = jnp.float32
+MESH = pl.DeviceIdType.MESH
+
+
+def dot_nn(left, right):
+    return lax.dot_general(left, right, (((1,), (0,)), ((), ())), preferred_element_type=F32)
+
+
+def dot_nt(left, right):
+    return lax.dot_general(left, right, (((1,), (1,)), ((), ())), preferred_element_type=F32)
+
+
+def shift_lanes(field, amount):
+    return pltpu.roll(field, amount, 1)
+
+
+def widen(field, lanes):
+    return jnp.concatenate(
+        [field, jnp.zeros((field.shape[0], lanes - field.shape[1]), field.dtype)], axis=1
+    )
+
+
+def fast_kernel(
+    n_dp,
+    n_ctx,
+    tok,
+    cot,
+    starts,
+    gains,
+    cos_ref,
+    sin_ref,
+    w_pack,
+    w_gate,
+    w_up,
+    w_down,
+    out_ref,
+    ig_ref,
+    gg_ref,
+    g_pack_ref,
+    g_gu_ref,
+    g_down_ref,
+    gb,
+    wt,
+    big,
+    wd,
+    na_ref,
+    qt,
+    kvb,
+    sc,
+    pp,
+    rl,
+    at,
+    resid_ref,
+    xb,
+    cb,
+    op,
+    orecv,
+    dn,
+    drecv,
+    dna,
+    hb,
+    dgu,
+    xt,
+    ht,
+    gres,
+    dat,
+    rb,
+    dkv,
+    dkv_r,
+    dkv_z,
+    kvsum,
+    gu_r,
+    gu_z,
+    gd,
+    gd_r,
+    gd_z,
+    g_r,
+    g_p,
+    g_z,
+    nat,
+    ggs,
+    gg_p,
+    gg_c,
+    s_send,
+    s_gain,
+    s_a,
+    s_ap,
+    s_b,
+    s_bz,
+    s_bp,
+    s_kv,
+    s_gu,
+    s_wd,
+    s_x,
+    s_c,
+    s_o,
+    s_d,
+    s_dkv,
+    s_gur,
+    s_gdr,
+    s_gdz,
+    s_gr,
+    s_gp,
+    s_gz,
+    s_ggp,
+    s_ggc,
+):
+    n_z = n_ctx // 2
+    rows_tok, model = tok.shape
+    shard_rows = w_pack.shape[0]
+    cq = model // n_dp
+    ck = 96
+    ffs = w_gate.shape[1]
+    rf = w_down.shape[0]
+    kvh = 6
+    group = 3
+    hs = HEAD_SIZE
+    gl = group * rows_tok
+    pack = w_pack.shape[1]
+    d = lax.axis_index("dp")
+    c = lax.axis_index("ctx")
+    k = lax.rem(c, 2)
+    z = c // 2
+    mate = c + 1 - 2 * k
+    my_down = pl.multiple_of(k * rf, 128)
+    its_down = pl.multiple_of((1 - k) * rf, 128)
+    pending = []
+    counter = [0]
+
+    def zc(i):
+        return 2 * lax.rem(z + i, n_z) + k
+
+    def dd_of(i):
+        return lax.rem(d + i, n_dp)
+
+    def rdma(src, dst, rsem, to_d, to_c):
+        ssem = s_send.at[counter[0]]
+        counter[0] += 1
+        copy = pltpu.make_async_remote_copy(
+            src_ref=src,
+            dst_ref=dst,
+            send_sem=ssem,
+            recv_sem=rsem,
+            device_id=(to_d, to_c),
+            device_id_type=MESH,
+        )
+        copy.start()
+        pending.append(copy)
+        return copy
+
+    def arrived(dst, rsem):
+        pltpu.make_async_remote_copy(
+            src_ref=dst,
+            dst_ref=dst,
+            send_sem=s_send.at[0],
+            recv_sem=rsem,
+            device_id=(d, mate),
+            device_id_type=MESH,
+        ).wait_recv()
+
+    wt[d, z, k] = w_pack[...]
+    gb[c] = gains[...]
+    la = pl.ds(0, 512)
+    lb = pl.ds(512, pack - 512)
+    for i in range(1, n_z):
+        rdma(wt.at[d, z, k, :, la], wt.at[d, z, k, :, la], s_a.at[0, n_z - i], d, zc(i))
+    for i in range(1, n_dp):
+        rdma(wt.at[d, z, k, :, la], wt.at[d, z, k, :, la], s_a.at[n_dp - i, 0], dd_of(i), c)
+    for i in range(1, n_ctx):
+        rdma(gb.at[c], gb.at[c], s_gain.at[n_ctx - i], d, lax.rem(c + i, n_ctx))
+    big[k, 0, z] = w_gate[...]
+    big[k, 1, z] = w_up[...]
+    own = n_dp - 1
+    cot_v = cot[...].astype(F32)
+    for e in range(n_dp):
+        turned = cot_v if e == 0 else shift_lanes(cot_v, model - cq * e)
+        cb[own, e] = turned[:, :384].astype(BF)
+    stream = tok[...].astype(F32)
+    inv1 = lax.rsqrt(jnp.mean(stream * stream, axis=1, keepdims=True) + norm_eps)
+
+    for q in (1, n_z - 1, 2):
+        zq = lax.rem(z + q, n_z)
+        arrived(wt.at[d, zq, k, :, la], s_a.at[0, q])
+        for i in range(1, n_dp):
+            rdma(
+                wt.at[d, zq, k, :, la], wt.at[d, zq, k, :, la], s_a.at[n_dp - i, q], dd_of(i), c
+            )
+    rdma(wt.at[d, :, k, :, la], wt.at[d, :, k, :, la], s_ap.at[0], d, mate)
+    for i in range(1, n_z):
+        rdma(wt.at[d, z, k, :, lb], wt.at[d, z, k, :, lb], s_bz.at[n_z - i], d, zc(i))
+    for r in range(1, n_dp):
+        dr = dd_of(r)
+        for q in range(n_z):
+            arrived(wt.at[dr, lax.rem(z + q, n_z), k, :, la], s_a.at[r, q])
+        rdma(wt.at[dr, :, k, :, la], wt.at[dr, :, k, :, la], s_ap.at[r], d, mate)
+
+    gain_all = jnp.zeros((8, model), F32)
+    for i in range(1, n_ctx):
+        arrived(gb.at[lax.rem(c + i, n_ctx)], s_gain.at[i])
+    for e in range(n_ctx):
+        piece = widen(gb[e], model)
+        gain_all = gain_all + (piece if e == 0 else shift_lanes(piece, shard_rows * e))
+    gain1 = gain_all[0:1]
+    gain2 = gain_all[1:2]
+    normed = (stream * inv1 * gain1).astype(BF)
+    na_ref[...] = normed
+
+    kt = kvsum
+    for r in range(n_dp):
+        arrived(wt.at[dd_of(r), :, 1 - k, :, la], s_ap.at[r])
+
+    def project(e, _):
+        w = wt[e, :, :, :, 0:512].reshape(model, 512)
+        o = dot_nn(na_ref[...], w)
+        o_t = jnp.transpose(o)
+        at[pl.ds(pl.multiple_of(e * cq, 32), cq), :] = o_t[:cq]
+        kt[pl.ds(pl.multiple_of(e * ck, 32), ck), :] = o_t[cq : cq + ck]
+        kt[pl.ds(pl.multiple_of(model // 3 + e * ck, 32), ck), :] = o_t[cq + ck : cq + 2 * ck]
+        return 0
+
+    lax.fori_loop(0, n_dp, project, 0)
+    cosine = cos_ref[...]
+    sine = sin_ref[...]
+    half = hs // 2
+
+    def turn(first, second):
+        return first * cosine - second * sine, second * cosine + first * sine
+
+    def turn_back(first, second):
+        return first * cosine + second * sine, second * cosine - first * sine
+
+    kvw = model // 3
+    for g in range(kvh):
+        lo, hi = turn(kt[g * hs : g * hs + half], kt[g * hs + half : (g + 1) * hs])
+        kvb[c, 128 * g : 128 * g + 64, :] = jnp.concatenate([lo, hi], axis=0).astype(BF)
+        kvb[c, 128 * g + 64 : 128 * g + 128, :] = kt[kvw + g * hs : kvw + (g + 1) * hs].astype(BF)
+    for i in range(1, n_z):
+        rdma(kvb.at[c], kvb.at[c], s_kv.at[n_z - i], d, zc(i))
+    rdma(kvb.at[c], kvb.at[c], s_kv.at[n_z], d, mate)
+    for h in range(kvh * group):
+        lo, hi = turn(at[h * hs : h * hs + half], at[h * hs + half : (h + 1) * hs])
+        low = jnp.concatenate([lo, hi], axis=0).astype(BF)
+        qt[h * hs : (h + 1) * hs, :] = (low.astype(F32) * 0.125).astype(BF)
+
+    for q in range(1, n_z):
+        zq = lax.rem(z + q, n_z)
+        arrived(wt.at[d, zq, k, :, lb], s_bz.at[q])
+    for i in range(1, n_dp):
+        rdma(wt.at[d, :, k, :, lb], wt.at[d, :, k, :, lb], s_b.at[n_dp - i], dd_of(i), c)
+    rdma(wt.at[d, :, k, :, lb], wt.at[d, :, k, :, lb], s_bp.at[0], d, mate)
+    big_sends = []
+    for i in range(1, n_z):
+        big_sends.append(
+            rdma(big.at[k, 0:2, z], big.at[k, 0:2, z], s_gu.at[n_z - i], d, zc(i))
+        )
+    for i in range(1, n_z):
+        rdma(w_down, wd.at[d, pl.ds(my_down, rf)], s_wd.at[d], z, zc(i))
+
+    @pl.when(d == z)
+    def _():
+        wd[d, pl.ds(my_down, rf), :] = w_down[...]
+
+    self_down = pltpu.make_async_remote_copy(
+        src_ref=w_down,
+        dst_ref=wd.at[d, pl.ds(my_down, rf)],
+        send_sem=s_send.at[counter[0]],
+        recv_sem=s_wd.at[d],
+        device_id=(z, c),
+        device_id_type=MESH,
+    )
+    counter[0] += 1
+
+    @pl.when(d != z)
+    def _():
+        self_down.start()
+
+    for i in range(1, n_dp):
+        rdma(cb.at[own], cb.at[n_dp - i - 1], s_c.at[n_dp - i - 1], dd_of(i), c)
+    for q in range(1, n_z):
+        arrived(kvb.at[zc(q)], s_kv.at[q])
+        rdma(kvb.at[zc(q)], kvb.at[zc(q)], s_kv.at[n_z + q], d, mate)
+    for r in range(1, n_dp):
+        dr = dd_of(r)
+        arrived(wt.at[dr, :, k, :, lb], s_b.at[r])
+        rdma(wt.at[dr, :, k, :, lb], wt.at[dr, :, k, :, lb], s_bp.at[r], d, mate)
+    for q in range(n_z):
+        arrived(kvb.at[2 * lax.rem(z + q, n_z) + 1 - k], s_kv.at[n_z + q])
+
+    tpos = c * rows_tok + lax.broadcasted_iota(jnp.int32, (1, rows_tok), 1)
+    lim = tpos
+    for p in range(PICS):
+        s_p = starts[0, p]
+        lim = jnp.where((tpos >= s_p) & (tpos < s_p + PIC), jnp.maximum(lim, s_p + PIC - 1), lim)
+    lim3 = jnp.concatenate([lim] * group, axis=1)
+
+    def heads_of(ref, g):
+        return jnp.concatenate(
+            [
+                ref[pl.ds(pl.multiple_of(g * group * hs + hs * j, hs), hs), :]
+                for j in range(group)
+            ],
+            axis=1,
+        )
+
+    def attend(g, _):
+        q_t = heads_of(qt, g)
+        q_z = jnp.concatenate([q_t, jnp.zeros_like(q_t)], axis=0)
+        k0 = pl.multiple_of(g * 128, 128)
+        most = jnp.full((1, gl), -1e30, F32)
+        for b in range(n_ctx):
+            kv = jnp.transpose(kvb[b, pl.ds(k0, 128), :])
+            s = dot_nn(kv, q_z)
+            kpos = b * rows_tok + lax.broadcasted_iota(jnp.int32, (rows_tok, gl), 0)
+            s = jnp.where(kpos <= lim3, s, -1e30)
+            sc[b * rows_tok : (b + 1) * rows_tok, :] = s
+            most = jnp.maximum(most, jnp.max(s, axis=0, keepdims=True))
+        total = jnp.zeros((1, gl), F32)
+        o_t = jnp.zeros((hs, gl), F32)
+        for b in range(n_ctx):
+            p = jnp.exp(sc[b * rows_tok : (b + 1) * rows_tok, :] - most)
+            p_low = p.astype(BF)
+            pp[g, b * rows_tok : (b + 1) * rows_tok, :] = p_low
+            total = total + jnp.sum(p, axis=0, keepdims=True)
+            o_t = o_t + dot_nn(kvb[b, pl.ds(pl.multiple_of(k0 + hs, hs), hs), :], p_low)
+        inv = 1.0 / total
+        rl[g] = jnp.broadcast_to(inv, (8, gl))
+        o_t = o_t * inv
+        for j in range(group):
+            at[pl.ds(pl.multiple_of(g * group * hs + hs * j, hs), hs), :] = o_t[
+                :, rows_tok * j : rows_tok * (j + 1)
+            ]
+        return 0
+
+    lax.fori_loop(0, kvh, attend, 0)
+
+    big_sends.append(rdma(big.at[k, 0:2, z], big.at[k, 0:2, z], s_gu.at[n_z], d, mate))
+    for q in range(1, n_z):
+        zq = lax.rem(z + q, n_z)
+        arrived(big.at[k, 0:2, zq], s_gu.at[q])
+        big_sends.append(
+            rdma(big.at[k, 0:2, zq], big.at[k, 0:2, zq], s_gu.at[n_z + q], d, mate)
+        )
+    for e in range(n_dp):
+
+        @pl.when((d != z) | (d != e))
+        def _():
+            arrived(wd.at[e, pl.ds(my_down, rf)], s_wd.at[e])
+
+    rdma(wd.at[:, pl.ds(my_down, rf)], wd.at[:, pl.ds(my_down, rf)], s_wd.at[n_dp], d, mate)
+
+    att_t = at[...].astype(BF)
+    nat[:, 0:rows_tok] = jnp.transpose(na_ref[...])
+    nat[:, rows_tok : 2 * rows_tok] = att_t
+    na_ref[...] = jnp.transpose(att_t)
+    resid_ref[...] = tok[...].astype(F32)
+    for r in range(n_dp):
+        arrived(wt.at[dd_of(r), :, 1 - k, :, lb], s_bp.at[r])
+    lead = 2 * ck + cq - 384
+
+    def out_block(e, _):
+        w = wt[e, :, :, :, 384:pack].reshape(model, pack - 384)
+        o = dot_nn(na_ref[...], w)
+        lane = lax.broadcasted_iota(jnp.int32, o.shape, 1)
+        o = widen(jnp.where(lane >= lead, o, 0.0), model)
+        resid_ref[...] += shift_lanes(o, lax.rem(e * cq + model - lead, model))
+        return 0
+
+    lax.fori_loop(0, n_dp, out_block, 0)
+    resid = resid_ref[...]
+    inv2 = lax.rsqrt(jnp.mean(resid * resid, axis=1, keepdims=True) + norm_eps)
+    xb[own] = (resid * inv2 * gain2).astype(BF)
+    for i in range(1, n_dp):
+        rdma(xb.at[own], xb.at[n_dp - i - 1], s_x.at[n_dp - i - 1], dd_of(i), c)
+    xt[:, own * rows_tok :] = jnp.transpose(xb[own])
+    for q in range(n_z):
+        arrived(big.at[1 - k, 0:2, lax.rem(z + q, n_z)], s_gu.at[n_z + q])
+    arrived(wd.at[:, pl.ds(its_down, rf)], s_wd.at[n_dp])
+    for p in range(n_dp - 1):
+        arrived(cb.at[p], s_c.at[p])
+    for p in range(n_dp - 1):
+        arrived(xb.at[p], s_x.at[p])
+
+    nc = 256
+
+    def weight_cols(e, n0):
+        return jnp.concatenate(
+            [big[b % 2, e, b // 2, :, pl.ds(n0, nc)] for b in range(n_ctx)], axis=0
+        )
+
+    for hf in range(n_dp // 2):
+        t0 = 2 * hf
+        r0 = t0 * rows_tok
+        rh = 2 * rows_tok
+        dna[...] = jnp.zeros_like(dna)
+
+        def cols(n, _):
+            n0 = pl.multiple_of(n * nc, nc)
+            n1 = pl.multiple_of(n * nc + ffs, nc)
+            x = xb[t0 : t0 + 2].reshape(rh, model)
+            w_g = weight_cols(0, n0)
+            w_u = weight_cols(1, n0)
+            g = dot_nn(x, w_g)
+            u = dot_nn(x, w_u)
+            dh = jnp.zeros((rh, nc), F32)
+            for e in range(n_dp):
+                dh = dh + dot_nt(cb[t0 : t0 + 2, e].reshape(rh, 384), wd[e, pl.ds(n0, nc), :])
+            sg = jax.nn.sigmoid(g)
+            si = g * sg
+            hb[r0 : r0 + rh, pl.ds(n0, nc)] = (si * u).astype(BF)
+            dg = (dh * u * sg * (1.0 + g * (1.0 - sg))).astype(BF)
+            du = (dh * si).astype(BF)
+            dgu[r0 : r0 + rh, pl.ds(n0, nc)] = dg
+            dgu[r0 : r0 + rh, pl.ds(n1, nc)] = du
+            dna[...] += dot_nt(dg, w_g) + dot_nt(du, w_u)
+            return 0
+
+        lax.fori_loop(0, ffs // nc, cols, 0)
+        dn[t0 : t0 + 2] = dna[...].astype(BF).reshape(2, rows_tok, model)
+        for p in (t0, t0 + 1):
+            if p != own:
+                there = n_dp - p - 2
+                rdma(dn.at[p], drecv.at[there], s_d.at[there], dd_of(p + 1), c)
+        for e in range(n_dp):
+            y = dot_nn(hb[r0 : r0 + rh, :], wd[e])
+            op[t0 : t0 + 2, e] = y.astype(BF).reshape(2, rows_tok, 384)
+        for p in (t0, t0 + 1):
+            if p != own:
+                there = n_dp - p - 2
+                rdma(op.at[p], orecv.at[there], s_o.at[there], dd_of(p + 1), c)
+
+    for p in range(n_dp - 1):
+        xt[:, p * rows_tok : (p + 1) * rows_tok] = jnp.transpose(xb[p])
+    for p in range(n_dp):
+        ht[:, p * rows_tok : (p + 1) * rows_tok] = jnp.transpose(
+            hb[p * rows_tok : (p + 1) * rows_tok, :]
+        )
+    for e in range(2):
+
+        def gu_cols(n, _):
+            n0 = pl.multiple_of(n * nc, nc)
+            n1 = pl.multiple_of(n * nc + e * ffs, nc)
+            r = dot_nn(xt[...], dgu[:, pl.ds(n1, nc)]).astype(BF)
+            for b in range(n_ctx):
+                big[b % 2, 2 + e, b // 2, :, pl.ds(n0, nc)] = r[
+                    shard_rows * b : shard_rows * (b + 1)
+                ]
+            return 0
+
+        lax.fori_loop(0, ffs // nc, gu_cols, 0)
+    big_sends.append(rdma(big.at[1 - k, 2:4], gu_r, s_gur.at[0], d, mate))
+
+    def gd_cols(e, _):
+        r = dot_nn(ht[...], cb[:, e].reshape(n_dp * rows_tok, 384)).astype(BF)
+        for j in range(2):
+            gd[j, e] = r[rf * j : rf * (j + 1)]
+        return 0
+
+    lax.fori_loop(0, n_dp, gd_cols, 0)
+    rdma(gd.at[1 - k], gd_r, s_gdr.at[0], d, mate)
+
+    for p in range(n_dp - 1):
+        arrived(drecv.at[p], s_d.at[p])
+    d_nm = dna[rows_tok : 2 * rows_tok, :]
+    for p in range(n_dp - 1):
+        d_nm = d_nm + drecv[p].astype(F32)
+
+    def norm_out(inputs, inverse, gain_vec, upstream):
+        scaled = gain_vec * upstream
+        return inverse * scaled - inputs * inverse * inverse * inverse * jnp.mean(
+            scaled * inputs, axis=1, keepdims=True
+        )
+
+    resid = resid_ref[...]
+    ggs[1:2, :] = jnp.sum(d_nm * resid * inv2, axis=0, keepdims=True)
+    d_res = cot[...].astype(F32) + norm_out(resid, inv2, gain2, d_nm)
+    gres[...] = d_res
+    d_low = d_res.astype(BF).astype(F32)
+    o0 = 2 * ck + cq
+    for e in range(n_dp):
+        t = shift_lanes(d_low, (o0 - cq * e) % model)[:, :pack]
+        lane = lax.broadcasted_iota(jnp.int32, t.shape, 1)
+        rb[e, rows_tok : 2 * rows_tok, :] = jnp.where(lane >= o0, t, 0.0).astype(BF)
+    dna[...] = jnp.zeros_like(dna)
+
+    def att_block(e, _):
+        w = wt[e, :, :, :, 384:pack].reshape(model, pack - 384)
+        dna[0:rows_tok, :] += dot_nt(rb[e, rows_tok : 2 * rows_tok, 384:pack], w)
+        return 0
+
+    lax.fori_loop(0, n_dp, att_block, 0)
+    dat[...] = jnp.transpose(dna[0:rows_tok, :].astype(BF))
+
+    arrived(gu_r, s_gur.at[0])
+
+    def gu_sum(n, _):
+        e = n // n_z
+        j = lax.rem(n, n_z)
+        gu_r[e, j] = (gu_r[e, j].astype(F32) + big[k, 2 + e, j].astype(F32)).astype(BF)
+        return 0
+
+    lax.fori_loop(0, 2 * n_z, gu_sum, 0)
+    for i in range(1, n_z):
+        there = n_z - i - 1
+        rdma(
+            gu_r.at[:, lax.rem(z + i, n_z)], gu_z.at[there], s_gur.at[there + 1], d, zc(i)
+        )
+    arrived(gd_r, s_gdr.at[0])
+
+    def gd_sum(e, _):
+        gd_r[e] = (gd_r[e].astype(F32) + gd[k, e].astype(F32)).astype(BF)
+        return 0
+
+    lax.fori_loop(0, n_dp, gd_sum, 0)
+    for i in range(1, n_dp):
+        rdma(gd_r.at[dd_of(i)], gd_z.at[z], s_gdz.at[z], dd_of(i), 2 * d + k)
+
+    @pl.when(d == z)
+    def _():
+        gd_z[z] = gd_r[d]
+
+    self_grad = pltpu.make_async_remote_copy(
+        src_ref=gd_r.at[d],
+        dst_ref=gd_z.at[z],
+        send_sem=s_send.at[counter[0]],
+        recv_sem=s_gdz.at[z],
+        device_id=(d, 2 * d + k),
+        device_id_type=MESH,
+    )
+    counter[0] += 1
+
+    @pl.when(d != z)
+    def _():
+        self_grad.start()
+
+    def attend_back(g, _):
+        q_t = heads_of(qt, g)
+        a_t = heads_of(dat, g)
+        o_t = heads_of(at, g)
+        none = jnp.zeros_like(q_t)
+        inv = rl[g][0:1]
+        delta = jnp.sum(a_t.astype(F32) * o_t, axis=0, keepdims=True) * inv
+        a_z = jnp.concatenate([none, a_t], axis=0)
+        a_inv = (a_t.astype(F32) * inv).astype(BF)
+        q2 = jnp.transpose(jnp.concatenate([q_t, none], axis=0))
+        a2 = jnp.transpose(jnp.concatenate([none, a_inv], axis=0))
+        k0 = pl.multiple_of(g * 128, 128)
+        dq = jnp.zeros((hs, gl), F32)
+        for b in range(n_ctx):
+            kv_t = kvb[b, pl.ds(k0, 128), :]
+            dp = dot_nn(jnp.transpose(kv_t), a_z)
+            p_low = pp[g, b * rows_tok : (b + 1) * rows_tok, :]
+            ds = (p_low.astype(F32) * (dp * inv - delta)).astype(BF)
+            dq = dq + dot_nn(kv_t[:hs], ds)
+            both = dot_nn(ds, q2) + dot_nn(p_low, a2)
+            dkv[b % 2, b // 2, pl.ds(k0, 128), :] = jnp.transpose(both).astype(BF)
+        dq = dq * 0.125
+        for j in range(group):
+            at[pl.ds(pl.multiple_of(g * group * hs + hs * j, hs), hs), :] = dq[
+                :, rows_tok * j : rows_tok * (j + 1)
+            ]
+        return 0
+
+    lax.fori_loop(0, kvh, attend_back, 0)
+    rdma(dkv.at[1 - k], dkv_r, s_dkv.at[0], d, mate)
+    for h in range(kvh * group):
+        lo, hi = turn_back(at[h * hs : h * hs + half], at[h * hs + half : (h + 1) * hs])
+        qt[h * hs : (h + 1) * hs, :] = jnp.concatenate([lo, hi], axis=0).astype(BF)
+    arrived(dkv_r, s_dkv.at[0])
+
+    def kv_sum(j, _):
+        dkv_r[j] = (dkv_r[j].astype(F32) + dkv[k, j].astype(F32)).astype(BF)
+        return 0
+
+    lax.fori_loop(0, n_z, kv_sum, 0)
+    for i in range(1, n_z):
+        there = n_z - i - 1
+        rdma(dkv_r.at[lax.rem(z + i, n_z)], dkv_z.at[there], s_dkv.at[there + 1], d, zc(i))
+
+    for p in range(n_dp - 1):
+        arrived(orecv.at[p], s_o.at[p])
+    y_all = resid_ref[...]
+    for e in range(n_dp):
+        y = op[own, e].astype(F32)
+        for p in range(n_dp - 1):
+            y = y + orecv[p, e].astype(F32)
+        y = widen(y, model)
+        y_all = y_all + (y if e == 0 else shift_lanes(y, cq * e))
+    out_ref[...] = y_all.astype(BF)
+    for copy in big_sends:
+        copy.wait_send()
+    pending[:] = [copy for copy in pending if all(copy is not other for other in big_sends)]
+
+    for i in range(n_z - 1):
+        arrived(dkv_z.at[i], s_dkv.at[i + 1])
+    kv_total = dkv_r[z].astype(F32)
+    for i in range(n_z - 1):
+        kv_total = kv_total + dkv_z[i].astype(F32)
+    kvsum[...] = kv_total
+    for g in range(kvh):
+        r = 128 * g
+        lo, hi = turn_back(kvsum[r : r + half], kvsum[r + half : r + hs])
+        at[g * hs : (g + 1) * hs, :] = jnp.concatenate([lo, hi], axis=0)
+        at[kvw + g * hs : kvw + (g + 1) * hs, :] = kvsum[r + hs : r + 2 * hs]
+    for e in range(n_dp):
+        rows = jnp.concatenate(
+            [
+                qt[cq * e : cq * (e + 1)],
+                at[ck * e : ck * (e + 1)].astype(BF),
+                at[kvw + ck * e : kvw + ck * (e + 1)].astype(BF),
+                jnp.zeros((512 - o0, rows_tok), BF),
+            ],
+            axis=0,
+        )
+        rb[e, 0:rows_tok, :] = widen(jnp.transpose(rows), pack)
+
+    for r in (1, 2, 3, 0):
+        e = dd_of(r)
+
+        def pack_cols(n, _):
+            n0 = pl.multiple_of(n * nc, nc)
+            t = dot_nn(nat[...], rb[e, :, pl.ds(n0, nc)]).astype(BF)
+            for b in range(n_ctx):
+                big[b % 2, e, b // 2, :, pl.ds(n0, nc)] = t[
+                    shard_rows * b : shard_rows * (b + 1)
+                ]
+            return 0
+
+        lax.fori_loop(0, pack // nc, pack_cols, 0)
+        rdma(big.at[1 - k, e], g_r.at[e], s_gr.at[r], d, mate)
+
+    def chip_sum(r):
+        e = dd_of(r)
+        arrived(g_r.at[e], s_gr.at[r])
+
+        def one(j, _):
+            g_r[e, j] = (g_r[e, j].astype(F32) + big[k, e, j].astype(F32)).astype(BF)
+            return 0
+
+        lax.fori_loop(0, n_z, one, 0)
+        return e
+
+    for r in range(1, n_dp):
+        e = chip_sum(r)
+        there = n_dp - r - 1
+        rdma(g_r.at[e], g_p.at[there], s_gp.at[there], e, c)
+
+    dna[...] = jnp.zeros_like(dna)
+
+    def in_block(e, _):
+        w = wt[e, :, :, :, 0:512].reshape(model, 512)
+        dna[0:rows_tok, :] += dot_nt(rb[e, 0:rows_tok, 0:512], w)
+        return 0
+
+    lax.fori_loop(0, n_dp, in_block, 0)
+    d_na = dna[0:rows_tok, :]
+    stream = tok[...].astype(F32)
+    ggs[0:1, :] = jnp.sum(d_na * stream * inv1, axis=0, keepdims=True)
+    ig_ref[...] = gres[...] + norm_out(stream, inv1, gain1, d_na)
+    for i in range(1, n_dp):
+        there = n_dp - i - 1
+        rdma(ggs, gg_p.at[there], s_ggp.at[there], dd_of(i), c)
+    chip_sum(0)
+    for p in range(n_dp - 1):
+        arrived(gg_p.at[p], s_ggp.at[p])
+    gg_all = ggs[...]
+    for p in range(n_dp - 1):
+        gg_all = gg_all + gg_p[p]
+    gg_c[0] = gg_all
+    for i in range(1, n_ctx):
+        rdma(gg_c.at[0], gg_c.at[n_ctx - i], s_ggc.at[n_ctx - i], d, lax.rem(c + i, n_ctx))
+    for i in range(n_z - 1):
+        arrived(gu_z.at[i], s_gur.at[i + 1])
+    for e in range(2):
+        t = gu_r[e, z].astype(F32)
+        for i in range(n_z - 1):
+            t = t + gu_z[i, e].astype(F32)
+        g_gu_ref[e] = t
+    for j in range(n_z):
+
+        @pl.when((d != z) | (z != j))
+        def _():
+            arrived(gd_z.at[j], s_gdz.at[j])
+
+    t = gd_z[0].astype(F32)
+    for j in range(1, n_z):
+        t = t + gd_z[j].astype(F32)
+    g_down_ref[...] = t
+    for p in range(n_dp - 1):
+        arrived(g_p.at[p], s_gp.at[p])
+
+    def plane_sum(j):
+        t = g_r[d, j].astype(F32)
+        for p in range(n_dp - 1):
+            t = t + g_p[p, j].astype(F32)
+        return t
+
+    for i in range(1, n_z):
+        zq = lax.rem(z + i, n_z)
+        there = n_z - i - 1
+        g_r[d, zq] = plane_sum(zq).astype(BF)
+        rdma(g_r.at[d, zq], g_z.at[there], s_gz.at[there], d, zc(i))
+    g_pack_ref[...] = plane_sum(z)
+    for i in range(1, n_ctx):
+        arrived(gg_c.at[i], s_ggc.at[i])
+    gg_tot = gg_c[0]
+    for i in range(1, n_ctx):
+        gg_tot = gg_tot + gg_c[i]
+    gg_ref[...] = shift_lanes(gg_tot, lax.rem(model - shard_rows * c, model))[:, :256]
+    for i in range(n_z - 1):
+        arrived(g_z.at[i], s_gz.at[i])
+    t = g_pack_ref[...]
+    for i in range(n_z - 1):
+        t = t + g_z[i].astype(F32)
+    g_pack_ref[...] = t
+    for copy in pending:
+        copy.wait_send()
+
+    @pl.when(d != z)
+    def _():
+        self_down.wait_send()
+        self_grad.wait_send()
+def fast_body(
+    n_dp,
+    n_ctx,
+    tokens,
+    starts,
+    gain_attn,
+    gain_mlp,
+    w_query,
+    w_key,
+    w_value,
+    w_out,
+    w_gate,
+    w_up,
+    w_down,
+    cotangent,
+):
+    n_z = n_ctx // 2
+    rows_tok, model = tokens.shape[1:]
+    sr = w_query.shape[0]
+    rf, cd = w_down.shape
+    ffs = w_gate.shape[1]
+    cq = w_query.shape[1]
+    ck = w_key.shape[1]
+    pack = 2 * (cq + ck)
+    length = rows_tok * n_ctx
+    gl = 3 * rows_tok
+    packed = jnp.concatenate([w_query, w_key, w_value, w_out], axis=1)
+    down = jnp.pad(w_down, ((0, 0), (0, 384 - cd)))
+    gains = jnp.pad(
+        jnp.stack([gain_attn, gain_mlp]).astype(jnp.float32), ((0, 6), (0, 256 - sr))
+    )
+    half = HEAD_SIZE // 2
+    positions = lax.axis_index("ctx") * rows_tok + jnp.arange(rows_tok)
+    freqs = 10000.0 ** (-jnp.arange(half).astype(jnp.float32) / half)
+    angles = freqs[:, None] * positions.astype(jnp.float32)[None, :]
+    vm = pl.BlockSpec(memory_space=pltpu.VMEM)
+    dma = pltpu.SemaphoreType.DMA
+    n = n_dp - 1
+    m = n_z - 1
+    scratch = [
+        pltpu.VMEM((n_ctx, 8, 256), F32),
+        pltpu.VMEM((n_dp, n_z, 2, sr, pack), BF),
+        pltpu.VMEM((2, n_dp, n_z, sr, ffs), BF),
+        pltpu.VMEM((n_dp, 2 * rf, 384), BF),
+        pltpu.VMEM((rows_tok, model), BF),
+        pltpu.VMEM((model, rows_tok), BF),
+        pltpu.VMEM((n_ctx, 2 * model // 3, rows_tok), BF),
+        pltpu.VMEM((length, gl), F32),
+        pltpu.VMEM((6, length, gl), BF),
+        pltpu.VMEM((6, 8, gl), F32),
+        pltpu.VMEM((model, rows_tok), F32),
+        pltpu.VMEM((rows_tok, model), F32),
+        pltpu.VMEM((n_dp, rows_tok, model), BF),
+        pltpu.VMEM((n_dp, n_dp, rows_tok, 384), BF),
+        pltpu.VMEM((n_dp, n_dp, rows_tok, 384), BF),
+        pltpu.VMEM((n, n_dp, rows_tok, 384), BF),
+        pltpu.VMEM((n_dp, rows_tok, model), BF),
+        pltpu.VMEM((n, rows_tok, model), BF),
+        pltpu.VMEM((2 * rows_tok, model), F32),
+        pltpu.VMEM((n_dp * rows_tok, ffs), BF),
+        pltpu.VMEM((n_dp * rows_tok, 2 * ffs), BF),
+        pltpu.VMEM((model, n_dp * rows_tok), BF),
+        pltpu.VMEM((ffs, n_dp * rows_tok), BF),
+        pltpu.VMEM((rows_tok, model), F32),
+        pltpu.VMEM((model, rows_tok), BF),
+        pltpu.VMEM((n_dp, 2 * rows_tok, pack), BF),
+        pltpu.VMEM((2, n_z, 2 * model // 3, rows_tok), BF),
+        pltpu.VMEM((n_z, 2 * model // 3, rows_tok), BF),
+        pltpu.VMEM((m, 2 * model // 3, rows_tok), BF),
+        pltpu.VMEM((2 * model // 3, rows_tok), F32),
+        pltpu.VMEM((2, n_z, sr, ffs), BF),
+        pltpu.VMEM((m, 2, sr, ffs), BF),
+        pltpu.VMEM((2, n_dp, rf, 384), BF),
+        pltpu.VMEM((n_dp, rf, 384), BF),
+        pltpu.VMEM((n_z, rf, 384), BF),
+        pltpu.VMEM((n_dp, n_z, sr, pack), BF),
+        pltpu.VMEM((n, n_z, sr, pack), BF),
+        pltpu.VMEM((m, sr, pack), BF),
+        pltpu.VMEM((model, 2 * rows_tok), BF),
+        pltpu.VMEM((8, model), F32),
+        pltpu.VMEM((n, 8, model), F32),
+        pltpu.VMEM((n_ctx, 8, model), F32),
+        dma((130,)),
+        dma((n_ctx,)),
+        dma((n_dp, n_z)),
+        dma((n_dp,)),
+        dma((n_dp,)),
+        dma((n_z,)),
+        dma((n_dp,)),
+        dma((2 * n_z,)),
+        dma((2 * n_z,)),
+        dma((n_dp + 1,)),
+        dma((n,)),
+        dma((n,)),
+        dma((n,)),
+        dma((n,)),
+        dma((n_z,)),
+        dma((n_z,)),
+        dma((1,)),
+        dma((n_z,)),
+        dma((n_dp,)),
+        dma((n,)),
+        dma((m,)),
+        dma((n,)),
+        dma((n_ctx,)),
+    ]
+    out, ig, gg, g_pack, g_gu, g_down = pl.pallas_call(
+        functools.partial(fast_kernel, n_dp, n_ctx),
+        out_shape=(
+            jax.ShapeDtypeStruct((rows_tok, model), BF),
+            jax.ShapeDtypeStruct((rows_tok, model), F32),
+            jax.ShapeDtypeStruct((8, 256), F32),
+            jax.ShapeDtypeStruct((sr, pack), F32),
+            jax.ShapeDtypeStruct((2, sr, ffs), F32),
+            jax.ShapeDtypeStruct((rf, 384), F32),
+        ),
+        in_specs=[vm, vm, pl.BlockSpec(memory_space=pltpu.SMEM)] + [vm] * 7,
+        out_specs=(vm,) * 6,
+        scratch_shapes=scratch,
+        compiler_params=pltpu.CompilerParams(
+            has_side_effects=True, vmem_limit_bytes=67043328
+        ),
+        name="layer",
+    )(
+        tokens[0],
+        cotangent[0],
+        starts,
+        gains,
+        jnp.cos(angles),
+        jnp.sin(angles),
+        packed,
+        w_gate,
+        w_up,
+        down,
+    )
+    return (
+        out[None],
+        ig[None],
+        gg[0, :sr],
+        gg[1, :sr],
+        g_pack[:, :cq],
+        g_pack[:, cq : cq + ck],
+        g_pack[:, cq + ck : cq + 2 * ck],
+        g_pack[:, cq + 2 * ck :],
+        g_gu[0],
+        g_gu[1],
+        g_down[:, :cd],
+    )
+
+
 def solution(mesh):
+    n_dp = mesh.shape["dp"]
+    n_ctx = mesh.shape["ctx"]
+
+    def choose(tokens, *rest):
+        fits = n_dp == 4 and n_ctx == 2 * n_dp and tokens.shape[1:] == (128, 1152)
+        if fits:
+            return fast_body(n_dp, n_ctx, tokens, *rest)
+        return body(tokens, *rest)
+
     return jax.shard_map(
-        body,
+        choose,
         mesh=mesh,
         in_specs=(
             P("dp", "ctx", None),

time: 652 us -> 381 us (0.58)
  waiting for transfers between devices: 373 us -> 0 us
  Pallas kernels: 0 us -> 360 us
  blocking collectives: 90.2 us -> 0 us
  local copies, waits for them, and re-layouts: 73.2 us -> 11.2 us
  matrix products: 55.7 us -> 0 us
  other arithmetic: 24.7 us -> 3.19 us
  between operations: 16.7 us -> 0.69 us
    pallas_call x0 -> x1, Pallas kernels: none -> 360 us  [fast_body(): pl.pallas_call(functools.partial(fast_kernel, n_dp, n_ctx), out_shape=(ja...]
    reduce_scatter x3 -> x0, waiting for transfers between devices: 182 us -> none  [the longest x1 112 us: body(): lax.psum_scatter(cut.reshape(-1, cut.shape[2]), ('dp', 'ctx'), scatter_di...]
    all_gather x6 -> x0, waiting for transfers between devices: 147 us -> none  [the longest x1 53.4 us: fetch_weights(): packed = lax.all_gather(packed, ('dp', 'ctx'), axis=0, tiled=True)]
    dot_general x28 -> x0, matrix products: 55.7 us -> none  [the longest x1 5.16 us: body(): jnp.einsum('td,fd->tf', cot_cols, mat_down, preferred_element_type=jnp.fl...]
    all_gather x3 -> x0, blocking collectives: 51.5 us -> none  [the longest x1 22.5 us: gather_keys(): lax.all_gather(key_rot, 'ctx', axis=0, tiled=True)]
    psum x1 -> x0, blocking collectives: 38.7 us -> none  [body(): lax.psum(jnp.stack([grad_gain_one, grad_gain_two]), ('dp', 'ctx'))]
    unnamed x15 -> x0, waiting for transfers between devices: 38.5 us -> none
    transpose x6 -> x0, local copies, waits for them, and re-layouts: 20.5 us -> none  [fetch_weights(): cuts.append(jnp.transpose(part, (1, 0, 2)).reshape(part.shape[1], -1))]
  transfers between devices with their start and end apart: 13 -> 0, of which waited for: 10 -> 0; matrix products, arithmetic and copies ran while one was open for 17% -> 0% of each run, Pallas kernels for 0% -> 0%
where the time goes in v2:
time: 381 us; the launch traced here: 375 us
  Pallas kernels  360 us (94%)
  local copies, waits for them, and re-layouts  11.2 us (3%)
    pallas_call x1, Pallas kernels, fast_body(): pl.pallas_call(functools.partial(fast_kernel, n_dp, n_ctx), out_shape=(ja...  360 us

profile of v2, /device:TPU:0, one launch (start us, length us, event | category | flops | bytes accessed | tf_op | source)
XLA Modules:
  0.0 374.8 jit_solution(9299276185603419222)
XLA Ops:
  0.6 0.0 copy-start.5
  0.7 0.7 stack.9
  1.3 0.7 stack.10
  2.0 0.6 fusion.6.gains
  2.6 0.8 multiply_sine_fusion
  3.4 0.0 copy-done.5
  3.4 0.0 copy-start.4
  3.4 1.8 pad_maximum_fusion.w_pack
  5.2 0.0 copy-done.4
  5.2 0.2 copy.23
  5.4 0.8 pad.12.w_down
  6.2 359.7 %layer.1 = (bf16[128,1152]{1,0:T(8,128)(2,1)}, f32[128,1152]{1,0:T(8,128)}, f32[8,256]{1,0:T(8,128)}, f32[144,768]{1,0:T(8,128)}, f32[2,144,768]{2,1,0:T(8,128)}, /*index=5*/f32[384,384]{1,0:T(8,128)}) custom-call(bf16[128,1152]{1,0:T(8,128)(2,1)} %bitcast.14, bf16[128,1152]{1,0:T(8,128)(2,1)} %bitcast.15, s32[1,4]{1,0:T(1,128)} %starts.1, ...), custom_call_target="tpu_custom_call" | custom-call | tf_op jit(solution)/shard_map/layer/pallas_call | solution.py:1239
  365.9 1.3 fusion.9
  367.2 0.0 copy-start.2
  367.2 1.7 fusion.8
  368.9 1.9 fusion.7
  370.9 0.0 copy-done.2
  370.9 1.0 copy.24
  371.8 0.0 copy-done
  371.9 1.0 slice_bitcast_fusion
  372.8 0.0 copy-done.3
  372.8 0.7 copy.27
  373.5 0.4 copy-done.1
  374.0 0.8 copy.28
  (5 shorter events, 0.0 us)
Async XLA Ops:
  0.6 2.7 copy-start.5
  3.4 1.8 copy-start.4
  367.2 3.6 copy-start.2
  368.9 2.9 copy-start
  371.8 1.0 copy-start.3
  372.8 1.2 copy-start.1

commit v3 on v2

--- a/solution.py
+++ b/solution.py
@@ -454,6 +454,7 @@
     wt,
     big,
     wd,
+    wdz,
     na_ref,
     qt,
     kvb,
@@ -472,7 +473,7 @@
     hb,
     dgu,
     xt,
-    ht,
+    ct,
     gres,
     dat,
     rb,
@@ -484,6 +485,7 @@
     gu_z,
     gd,
     gd_r,
+    gd_p,
     gd_z,
     g_r,
     g_p,
@@ -502,6 +504,7 @@
     s_kv,
     s_gu,
     s_wd,
+    s_wdz,
     s_x,
     s_c,
     s_o,
@@ -509,6 +512,7 @@
     s_dkv,
     s_gur,
     s_gdr,
+    s_gdp,
     s_gdz,
     s_gr,
     s_gp,
@@ -522,7 +526,7 @@
     cq = model // n_dp
     ck = 96
     ffs = w_gate.shape[1]
-    rf = w_down.shape[0]
+    rf = w_down.shape[1]
     kvh = 6
     group = 3
     hs = HEAD_SIZE
@@ -535,6 +539,7 @@
     mate = c + 1 - 2 * k
     my_down = pl.multiple_of(k * rf, 128)
     its_down = pl.multiple_of((1 - k) * rf, 128)
+    big_sends = []
     pending = []
     counter = [0]
 
@@ -581,11 +586,23 @@
         rdma(gb.at[c], gb.at[c], s_gain.at[n_ctx - i], d, lax.rem(c + i, n_ctx))
     big[k, 0, z] = w_gate[...]
     big[k, 1, z] = w_up[...]
+    wdz[z] = w_down[...]
     own = n_dp - 1
-    cot_v = cot[...].astype(F32)
-    for e in range(n_dp):
-        turned = cot_v if e == 0 else shift_lanes(cot_v, model - cq * e)
-        cb[own, e] = turned[:, :384].astype(BF)
+    cb[own] = cot[...]
+
+    def down_rows(e):
+        return pl.ds(pl.multiple_of(e * cq, 32), cq)
+
+    def spread_rows(e):
+        for i in range(1, n_z):
+            copy = rdma(big.at[k, e, z], big.at[k, e, z], s_gu.at[e, n_z - i], d, zc(i))
+            big_sends.append(copy)
+
+    for i in range(1, n_z):
+        rdma(wt.at[d, z, k, :, lb], wt.at[d, z, k, :, lb], s_bz.at[n_z - i], d, zc(i))
+    for i in range(1, n_z):
+        rdma(wdz.at[z], wdz.at[z], s_wdz.at[n_z - i], d, zc(i))
+    spread_rows(0)
     stream = tok[...].astype(F32)
     inv1 = lax.rsqrt(jnp.mean(stream * stream, axis=1, keepdims=True) + norm_eps)
 
@@ -597,8 +614,6 @@
                 wt.at[d, zq, k, :, la], wt.at[d, zq, k, :, la], s_a.at[n_dp - i, q], dd_of(i), c
             )
     rdma(wt.at[d, :, k, :, la], wt.at[d, :, k, :, la], s_ap.at[0], d, mate)
-    for i in range(1, n_z):
-        rdma(wt.at[d, z, k, :, lb], wt.at[d, z, k, :, lb], s_bz.at[n_z - i], d, zc(i))
     for r in range(1, n_dp):
         dr = dd_of(r)
         for q in range(n_z):
@@ -648,6 +663,7 @@
     for i in range(1, n_z):
         rdma(kvb.at[c], kvb.at[c], s_kv.at[n_z - i], d, zc(i))
     rdma(kvb.at[c], kvb.at[c], s_kv.at[n_z], d, mate)
+    spread_rows(1)
     for h in range(kvh * group):
         lo, hi = turn(at[h * hs : h * hs + half], at[h * hs + half : (h + 1) * hs])
         low = jnp.concatenate([lo, hi], axis=0).astype(BF)
@@ -659,32 +675,12 @@
     for i in range(1, n_dp):
         rdma(wt.at[d, :, k, :, lb], wt.at[d, :, k, :, lb], s_b.at[n_dp - i], dd_of(i), c)
     rdma(wt.at[d, :, k, :, lb], wt.at[d, :, k, :, lb], s_bp.at[0], d, mate)
-    big_sends = []
-    for i in range(1, n_z):
-        big_sends.append(
-            rdma(big.at[k, 0:2, z], big.at[k, 0:2, z], s_gu.at[n_z - i], d, zc(i))
-        )
-    for i in range(1, n_z):
-        rdma(w_down, wd.at[d, pl.ds(my_down, rf)], s_wd.at[d], z, zc(i))
-
-    @pl.when(d == z)
-    def _():
-        wd[d, pl.ds(my_down, rf), :] = w_down[...]
-
-    self_down = pltpu.make_async_remote_copy(
-        src_ref=w_down,
-        dst_ref=wd.at[d, pl.ds(my_down, rf)],
-        send_sem=s_send.at[counter[0]],
-        recv_sem=s_wd.at[d],
-        device_id=(z, c),
-        device_id_type=MESH,
-    )
-    counter[0] += 1
-
-    @pl.when(d != z)
-    def _():
-        self_down.start()
-
+    for q in range(1, n_z):
+        arrived(wdz.at[lax.rem(z + q, n_z)], s_wdz.at[q])
+    for i in range(1, n_dp):
+        e = dd_of(i)
+        rdma(wdz.at[e], wd.at[down_rows(d), pl.ds(my_down, rf)], s_wd.at[n_dp - i], e, c)
+    wd[down_rows(d), pl.ds(my_down, rf)] = wdz[d]
     for i in range(1, n_dp):
         rdma(cb.at[own], cb.at[n_dp - i - 1], s_c.at[n_dp - i - 1], dd_of(i), c)
     for q in range(1, n_z):
@@ -744,20 +740,17 @@
 
     lax.fori_loop(0, kvh, attend, 0)
 
-    big_sends.append(rdma(big.at[k, 0:2, z], big.at[k, 0:2, z], s_gu.at[n_z], d, mate))
-    for q in range(1, n_z):
-        zq = lax.rem(z + q, n_z)
-        arrived(big.at[k, 0:2, zq], s_gu.at[q])
-        big_sends.append(
-            rdma(big.at[k, 0:2, zq], big.at[k, 0:2, zq], s_gu.at[n_z + q], d, mate)
-        )
-    for e in range(n_dp):
-
-        @pl.when((d != z) | (d != e))
-        def _():
-            arrived(wd.at[e, pl.ds(my_down, rf)], s_wd.at[e])
-
-    rdma(wd.at[:, pl.ds(my_down, rf)], wd.at[:, pl.ds(my_down, rf)], s_wd.at[n_dp], d, mate)
+    for r in range(1, n_dp):
+        arrived(wd.at[down_rows(dd_of(r)), pl.ds(my_down, rf)], s_wd.at[r])
+    rdma(wd.at[:, pl.ds(my_down, rf)], wd.at[:, pl.ds(my_down, rf)], s_wd.at[0], d, mate)
+    for e in range(2):
+        copy = rdma(big.at[k, e, z], big.at[k, e, z], s_gu.at[e, n_z], d, mate)
+        big_sends.append(copy)
+        for q in range(1, n_z):
+            zq = lax.rem(z + q, n_z)
+            arrived(big.at[k, e, zq], s_gu.at[e, q])
+            copy = rdma(big.at[k, e, zq], big.at[k, e, zq], s_gu.at[e, n_z + q], d, mate)
+            big_sends.append(copy)
 
     att_t = at[...].astype(BF)
     nat[:, 0:rows_tok] = jnp.transpose(na_ref[...])
@@ -783,11 +776,14 @@
     for i in range(1, n_dp):
         rdma(xb.at[own], xb.at[n_dp - i - 1], s_x.at[n_dp - i - 1], dd_of(i), c)
     xt[:, own * rows_tok :] = jnp.transpose(xb[own])
-    for q in range(n_z):
-        arrived(big.at[1 - k, 0:2, lax.rem(z + q, n_z)], s_gu.at[n_z + q])
-    arrived(wd.at[:, pl.ds(its_down, rf)], s_wd.at[n_dp])
     for p in range(n_dp - 1):
         arrived(cb.at[p], s_c.at[p])
+    for p in range(n_dp):
+        ct[:, p * rows_tok : (p + 1) * rows_tok] = jnp.transpose(cb[p])
+    for e in range(2):
+        for q in range(n_z):
+            arrived(big.at[1 - k, e, lax.rem(z + q, n_z)], s_gu.at[e, n_z + q])
+    arrived(wd.at[:, pl.ds(its_down, rf)], s_wd.at[0])
     for p in range(n_dp - 1):
         arrived(xb.at[p], s_x.at[p])
 
@@ -812,9 +808,7 @@
             w_u = weight_cols(1, n0)
             g = dot_nn(x, w_g)
             u = dot_nn(x, w_u)
-            dh = jnp.zeros((rh, nc), F32)
-            for e in range(n_dp):
-                dh = dh + dot_nt(cb[t0 : t0 + 2, e].reshape(rh, 384), wd[e, pl.ds(n0, nc), :])
+            dh = dot_nn(cb[t0 : t0 + 2].reshape(rh, model), wd[:, pl.ds(n0, nc)])
             sg = jax.nn.sigmoid(g)
             si = g * sg
             hb[r0 : r0 + rh, pl.ds(n0, nc)] = (si * u).astype(BF)
@@ -831,9 +825,8 @@
             if p != own:
                 there = n_dp - p - 2
                 rdma(dn.at[p], drecv.at[there], s_d.at[there], dd_of(p + 1), c)
-        for e in range(n_dp):
-            y = dot_nn(hb[r0 : r0 + rh, :], wd[e])
-            op[t0 : t0 + 2, e] = y.astype(BF).reshape(2, rows_tok, 384)
+        y = dot_nt(hb[r0 : r0 + rh, :], wd[...])
+        op[t0 : t0 + 2] = y.astype(BF).reshape(2, rows_tok, model)
         for p in (t0, t0 + 1):
             if p != own:
                 there = n_dp - p - 2
@@ -841,10 +834,6 @@
 
     for p in range(n_dp - 1):
         xt[:, p * rows_tok : (p + 1) * rows_tok] = jnp.transpose(xb[p])
-    for p in range(n_dp):
-        ht[:, p * rows_tok : (p + 1) * rows_tok] = jnp.transpose(
-            hb[p * rows_tok : (p + 1) * rows_tok, :]
-        )
     for e in range(2):
 
         def gu_cols(n, _):
@@ -860,13 +849,13 @@
         lax.fori_loop(0, ffs // nc, gu_cols, 0)
     big_sends.append(rdma(big.at[1 - k, 2:4], gu_r, s_gur.at[0], d, mate))
 
-    def gd_cols(e, _):
-        r = dot_nn(ht[...], cb[:, e].reshape(n_dp * rows_tok, 384)).astype(BF)
-        for j in range(2):
-            gd[j, e] = r[rf * j : rf * (j + 1)]
+    def gd_cols(j, _):
+        r = dot_nn(ct[...], hb[:, pl.ds(pl.multiple_of(j * rf, 128), rf)]).astype(BF)
+        for e in range(n_dp):
+            gd[j, e] = r[cq * e : cq * (e + 1)]
         return 0
 
-    lax.fori_loop(0, n_dp, gd_cols, 0)
+    lax.fori_loop(0, 2, gd_cols, 0)
     rdma(gd.at[1 - k], gd_r, s_gdr.at[0], d, mate)
 
     for p in range(n_dp - 1):
@@ -923,25 +912,71 @@
 
     lax.fori_loop(0, n_dp, gd_sum, 0)
     for i in range(1, n_dp):
-        rdma(gd_r.at[dd_of(i)], gd_z.at[z], s_gdz.at[z], dd_of(i), 2 * d + k)
-
-    @pl.when(d == z)
-    def _():
-        gd_z[z] = gd_r[d]
-
-    self_grad = pltpu.make_async_remote_copy(
-        src_ref=gd_r.at[d],
-        dst_ref=gd_z.at[z],
-        send_sem=s_send.at[counter[0]],
-        recv_sem=s_gdz.at[z],
-        device_id=(d, 2 * d + k),
-        device_id_type=MESH,
-    )
-    counter[0] += 1
-
-    @pl.when(d != z)
-    def _():
-        self_grad.start()
+        rdma(gd_r.at[dd_of(i)], gd_p.at[d], s_gdp.at[n_dp - i], dd_of(i), c)
+    gd_p[d] = gd_r[d]
+
+    for copy in big_sends:
+        copy.wait_send()
+    pending[:] = [copy for copy in pending if all(copy is not other for other in big_sends)]
+
+    def store_pack(e, n0, t):
+        for b in range(n_ctx):
+            big[b % 2, e, b // 2, :, pl.ds(n0, nc)] = t[shard_rows * b : shard_rows * (b + 1)]
+
+    def chip_sum(r, s, lanes):
+        e = dd_of(r)
+        arrived(g_r.at[e, :, :, lanes], s_gr.at[s, r])
+
+        def one(j, _):
+            mine = big[k, e, j, :, lanes].astype(F32)
+            g_r[e, j, :, lanes] = (g_r[e, j, :, lanes].astype(F32) + mine).astype(BF)
+            return 0
+
+        lax.fori_loop(0, n_z, one, 0)
+        return e
+
+    def to_plane(s, lanes):
+        for r in range(1, n_dp):
+            e = chip_sum(r, s, lanes)
+            there = n_dp - r - 1
+            rdma(
+                g_r.at[e, :, :, lanes], g_p.at[there, :, :, lanes], s_gp.at[s, there], e, c
+            )
+
+    def plane_sum(j, lanes):
+        t = g_r[d, j, :, lanes].astype(F32)
+        for p in range(n_dp - 1):
+            t = t + g_p[p, j, :, lanes].astype(F32)
+        return t
+
+    def to_z(s, lanes):
+        for p in range(n_dp - 1):
+            arrived(g_p.at[p, :, :, lanes], s_gp.at[s, p])
+        for i in range(1, n_z):
+            zq = lax.rem(z + i, n_z)
+            there = n_z - i - 1
+            g_r[d, zq, :, lanes] = plane_sum(zq, lanes).astype(BF)
+            rdma(
+                g_r.at[d, zq, :, lanes], g_z.at[there, :, lanes], s_gz.at[s, there], d, zc(i)
+            )
+        g_pack_ref[:, lanes] = plane_sum(z, lanes)
+
+    def last_sum(s, lanes):
+        for i in range(n_z - 1):
+            arrived(g_z.at[i, :, lanes], s_gz.at[s, i])
+        t = g_pack_ref[:, lanes]
+        for i in range(n_z - 1):
+            t = t + g_z[i, :, lanes].astype(F32)
+        g_pack_ref[:, lanes] = t
+
+    for r in (1, 2, 3, 0):
+        e = dd_of(r)
+        t = dot_nn(
+            nat[:, rows_tok : 2 * rows_tok], rb[e, rows_tok : 2 * rows_tok, 512:pack]
+        ).astype(BF)
+        store_pack(e, 512, t)
+        rdma(big.at[1 - k, e, :, :, lb], g_r.at[e, :, :, lb], s_gr.at[1, r], d, mate)
+    to_plane(1, lb)
 
     def attend_back(g, _):
         q_t = heads_of(qt, g)
@@ -986,20 +1021,20 @@
     for i in range(1, n_z):
         there = n_z - i - 1
         rdma(dkv_r.at[lax.rem(z + i, n_z)], dkv_z.at[there], s_dkv.at[there + 1], d, zc(i))
+    chip_sum(0, 1, lb)
+    to_z(1, lb)
+    for r in range(1, n_dp):
+        arrived(gd_p.at[dd_of(r)], s_gdp.at[r])
+    for i in range(1, n_z):
+        there = n_z - i - 1
+        rdma(gd_p.at[lax.rem(z + i, n_z)], gd_z.at[there], s_gdz.at[there], d, zc(i))
 
     for p in range(n_dp - 1):
         arrived(orecv.at[p], s_o.at[p])
-    y_all = resid_ref[...]
-    for e in range(n_dp):
-        y = op[own, e].astype(F32)
-        for p in range(n_dp - 1):
-            y = y + orecv[p, e].astype(F32)
-        y = widen(y, model)
-        y_all = y_all + (y if e == 0 else shift_lanes(y, cq * e))
+    y_all = resid_ref[...] + op[own].astype(F32)
+    for p in range(n_dp - 1):
+        y_all = y_all + orecv[p].astype(F32)
     out_ref[...] = y_all.astype(BF)
-    for copy in big_sends:
-        copy.wait_send()
-    pending[:] = [copy for copy in pending if all(copy is not other for other in big_sends)]
 
     for i in range(n_z - 1):
         arrived(dkv_z.at[i], s_dkv.at[i + 1])
@@ -1029,31 +1064,13 @@
 
         def pack_cols(n, _):
             n0 = pl.multiple_of(n * nc, nc)
-            t = dot_nn(nat[...], rb[e, :, pl.ds(n0, nc)]).astype(BF)
-            for b in range(n_ctx):
-                big[b % 2, e, b // 2, :, pl.ds(n0, nc)] = t[
-                    shard_rows * b : shard_rows * (b + 1)
-                ]
+            store_pack(e, n0, dot_nn(nat[...], rb[e, :, pl.ds(n0, nc)]).astype(BF))
             return 0
 
-        lax.fori_loop(0, pack // nc, pack_cols, 0)
-        rdma(big.at[1 - k, e], g_r.at[e], s_gr.at[r], d, mate)
-
-    def chip_sum(r):
-        e = dd_of(r)
-        arrived(g_r.at[e], s_gr.at[r])
-
-        def one(j, _):
-            g_r[e, j] = (g_r[e, j].astype(F32) + big[k, e, j].astype(F32)).astype(BF)
-            return 0
-
-        lax.fori_loop(0, n_z, one, 0)
-        return e
-
-    for r in range(1, n_dp):
-        e = chip_sum(r)
-        there = n_dp - r - 1
-        rdma(g_r.at[e], g_p.at[there], s_gp.at[there], e, c)
+        lax.fori_loop(0, 512 // nc, pack_cols, 0)
+        rdma(big.at[1 - k, e, :, :, la], g_r.at[e, :, :, la], s_gr.at[0, r], d, mate)
+
+    to_plane(0, la)
 
     dna[...] = jnp.zeros_like(dna)
 
@@ -1070,7 +1087,7 @@
     for i in range(1, n_dp):
         there = n_dp - i - 1
         rdma(ggs, gg_p.at[there], s_ggp.at[there], dd_of(i), c)
-    chip_sum(0)
+    chip_sum(0, 0, la)
     for p in range(n_dp - 1):
         arrived(gg_p.at[p], s_ggp.at[p])
     gg_all = ggs[...]
@@ -1086,50 +1103,23 @@
         for i in range(n_z - 1):
             t = t + gu_z[i, e].astype(F32)
         g_gu_ref[e] = t
-    for j in range(n_z):
-
-        @pl.when((d != z) | (z != j))
-        def _():
-            arrived(gd_z.at[j], s_gdz.at[j])
-
-    t = gd_z[0].astype(F32)
-    for j in range(1, n_z):
-        t = t + gd_z[j].astype(F32)
+    for i in range(n_z - 1):
+        arrived(gd_z.at[i], s_gdz.at[i])
+    t = gd_p[z].astype(F32)
+    for i in range(n_z - 1):
+        t = t + gd_z[i].astype(F32)
     g_down_ref[...] = t
-    for p in range(n_dp - 1):
-        arrived(g_p.at[p], s_gp.at[p])
-
-    def plane_sum(j):
-        t = g_r[d, j].astype(F32)
-        for p in range(n_dp - 1):
-            t = t + g_p[p, j].astype(F32)
-        return t
-
-    for i in range(1, n_z):
-        zq = lax.rem(z + i, n_z)
-        there = n_z - i - 1
-        g_r[d, zq] = plane_sum(zq).astype(BF)
-        rdma(g_r.at[d, zq], g_z.at[there], s_gz.at[there], d, zc(i))
-    g_pack_ref[...] = plane_sum(z)
+    last_sum(1, lb)
+    to_z(0, la)
     for i in range(1, n_ctx):
         arrived(gg_c.at[i], s_ggc.at[i])
     gg_tot = gg_c[0]
     for i in range(1, n_ctx):
         gg_tot = gg_tot + gg_c[i]
     gg_ref[...] = shift_lanes(gg_tot, lax.rem(model - shard_rows * c, model))[:, :256]
-    for i in range(n_z - 1):
-        arrived(g_z.at[i], s_gz.at[i])
-    t = g_pack_ref[...]
-    for i in range(n_z - 1):
-        t = t + g_z[i].astype(F32)
-    g_pack_ref[...] = t
+    last_sum(0, la)
     for copy in pending:
         copy.wait_send()
-
-    @pl.when(d != z)
-    def _():
-        self_down.wait_send()
-        self_grad.wait_send()
 def fast_body(
     n_dp,
     n_ctx,
@@ -1157,7 +1147,7 @@
     length = rows_tok * n_ctx
     gl = 3 * rows_tok
     packed = jnp.concatenate([w_query, w_key, w_value, w_out], axis=1)
-    down = jnp.pad(w_down, ((0, 0), (0, 384 - cd)))
+    down = jnp.transpose(w_down)
     gains = jnp.pad(
         jnp.stack([gain_attn, gain_mlp]).astype(jnp.float32), ((0, 6), (0, 256 - sr))
     )
@@ -1173,7 +1163,8 @@
         pltpu.VMEM((n_ctx, 8, 256), F32),
         pltpu.VMEM((n_dp, n_z, 2, sr, pack), BF),
         pltpu.VMEM((2, n_dp, n_z, sr, ffs), BF),
-        pltpu.VMEM((n_dp, 2 * rf, 384), BF),
+        pltpu.VMEM((model, 2 * rf), BF),
+        pltpu.VMEM((n_z, cd, rf), BF),
         pltpu.VMEM((rows_tok, model), BF),
         pltpu.VMEM((model, rows_tok), BF),
         pltpu.VMEM((n_ctx, 2 * model // 3, rows_tok), BF),
@@ -1183,16 +1174,16 @@
         pltpu.VMEM((model, rows_tok), F32),
         pltpu.VMEM((rows_tok, model), F32),
         pltpu.VMEM((n_dp, rows_tok, model), BF),
-        pltpu.VMEM((n_dp, n_dp, rows_tok, 384), BF),
-        pltpu.VMEM((n_dp, n_dp, rows_tok, 384), BF),
-        pltpu.VMEM((n, n_dp, rows_tok, 384), BF),
+        pltpu.VMEM((n_dp, rows_tok, model), BF),
+        pltpu.VMEM((n_dp, rows_tok, model), BF),
+        pltpu.VMEM((n, rows_tok, model), BF),
         pltpu.VMEM((n_dp, rows_tok, model), BF),
         pltpu.VMEM((n, rows_tok, model), BF),
         pltpu.VMEM((2 * rows_tok, model), F32),
         pltpu.VMEM((n_dp * rows_tok, ffs), BF),
         pltpu.VMEM((n_dp * rows_tok, 2 * ffs), BF),
         pltpu.VMEM((model, n_dp * rows_tok), BF),
-        pltpu.VMEM((ffs, n_dp * rows_tok), BF),
+        pltpu.VMEM((model, n_dp * rows_tok), BF),
         pltpu.VMEM((rows_tok, model), F32),
         pltpu.VMEM((model, rows_tok), BF),
         pltpu.VMEM((n_dp, 2 * rows_tok, pack), BF),
@@ -1202,9 +1193,10 @@
         pltpu.VMEM((2 * model // 3, rows_tok), F32),
         pltpu.VMEM((2, n_z, sr, ffs), BF),
         pltpu.VMEM((m, 2, sr, ffs), BF),
-        pltpu.VMEM((2, n_dp, rf, 384), BF),
-        pltpu.VMEM((n_dp, rf, 384), BF),
-        pltpu.VMEM((n_z, rf, 384), BF),
+        pltpu.VMEM((2, n_dp, cd, rf), BF),
+        pltpu.VMEM((n_dp, cd, rf), BF),
+        pltpu.VMEM((n_dp, cd, rf), BF),
+        pltpu.VMEM((m, cd, rf), BF),
         pltpu.VMEM((n_dp, n_z, sr, pack), BF),
         pltpu.VMEM((n, n_z, sr, pack), BF),
         pltpu.VMEM((m, sr, pack), BF),
@@ -1212,7 +1204,7 @@
         pltpu.VMEM((8, model), F32),
         pltpu.VMEM((n, 8, model), F32),
         pltpu.VMEM((n_ctx, 8, model), F32),
-        dma((130,)),
+        dma((150,)),
         dma((n_ctx,)),
         dma((n_dp, n_z)),
         dma((n_dp,)),
@@ -1220,8 +1212,9 @@
         dma((n_z,)),
         dma((n_dp,)),
         dma((2 * n_z,)),
-        dma((2 * n_z,)),
-        dma((n_dp + 1,)),
+        dma((2, 2 * n_z)),
+        dma((n_dp,)),
+        dma((n_z,)),
         dma((n,)),
         dma((n,)),
         dma((n,)),
@@ -1229,10 +1222,11 @@
         dma((n_z,)),
         dma((n_z,)),
         dma((1,)),
-        dma((n_z,)),
         dma((n_dp,)),
-        dma((n,)),
         dma((m,)),
+        dma((2, n_dp)),
+        dma((2, n)),
+        dma((2, m)),
         dma((n,)),
         dma((n_ctx,)),
     ]
@@ -1244,7 +1238,7 @@
             jax.ShapeDtypeStruct((8, 256), F32),
             jax.ShapeDtypeStruct((sr, pack), F32),
             jax.ShapeDtypeStruct((2, sr, ffs), F32),
-            jax.ShapeDtypeStruct((rf, 384), F32),
+            jax.ShapeDtypeStruct((cd, rf), F32),
         ),
         in_specs=[vm, vm, pl.BlockSpec(memory_space=pltpu.SMEM)] + [vm] * 7,
         out_specs=(vm,) * 6,
@@ -1276,7 +1270,7 @@
         g_pack[:, cq + 2 * ck :],
         g_gu[0],
         g_gu[1],
-        g_down[:, :cd],
+        jnp.transpose(g_down),
     )
 
 

time: 381 us -> 288 us (0.76); the launches traced: 375 us -> 287 us
  Pallas kernels: 360 us -> 273 us
    pallas_call x1, Pallas kernels: 360 us -> 273 us  [fast_body(): pl.pallas_call(functools.partial(fast_kernel, n_dp, n_ctx), out_shape=(ja...]
where the time goes in v3:
time: 288 us; the launch traced here: 287 us
  Pallas kernels  273 us (95%)
  local copies, waits for them, and re-layouts  10.3 us (4%)
  other arithmetic  3.15 us (1%)
    pallas_call x1, Pallas kernels, fast_body(): pl.pallas_call(functools.partial(fast_kernel, n_dp, n_ctx), out_shape=(ja...  273 us

profile of v3, /device:TPU:0, one launch (start us, length us, event | category | flops | bytes accessed | tf_op | source)
XLA Modules:
  0.0 287.0 jit_solution(11170107775349585205)
XLA Ops:
  0.6 0.0 copy-start.4
  0.7 0.7 stack.9
  1.3 0.7 stack.10
  2.0 0.6 fusion.6.gains
  2.6 0.8 multiply_sine_fusion
  3.4 0.0 copy-done.4
  3.4 1.8 pad_maximum_fusion.w_pack
  5.1 272.8 %layer.1 = (bf16[128,1152]{1,0:T(8,128)(2,1)}, f32[128,1152]{1,0:T(8,128)}, f32[8,256]{1,0:T(8,128)}, f32[144,768]{1,0:T(8,128)}, f32[2,144,768]{2,1,0:T(8,128)}, /*index=5*/f32[288,384]{1,0:T(8,128)}) custom-call(bf16[128,1152]{1,0:T(8,128)(2,1)} %bitcast.15, bf16[128,1152]{1,0:T(8,128)(2,1)} %bitcast.16, s32[1,4]{1,0:T(1,128)} %starts.1, ...), custom_call_target="tpu_custom_call" | custom-call | tf_op jit(solution)/shard_map/layer/pallas_call | solution.py:1233
  278.0 0.0 copy-start
  278.0 1.4 fusion.9
  279.3 1.6 fusion.8
  281.0 1.9 fusion.7
  282.8 0.0 copy-done
  282.8 0.0 copy-start.3
  282.8 1.0 slice_bitcast_fusion
  283.8 0.0 copy-start.1
  283.8 0.0 copy-done.3
  283.8 0.7 copy.26
  284.5 0.4 copy-done.1
  285.0 0.0 copy-start.2
  285.0 0.8 copy.27
  285.8 0.4 copy-done.2
  286.2 0.8 copy.28
  (2 shorter events, 0.0 us)
Async XLA Ops:
  0.6 2.7 copy-start.4
  278.0 4.9 %copy-start = (f32[2,144,768]{2,1,0:T(8,128)S(1)}, f32[2,144,768]{2,1,0:T(8,128)}, u32[]{:S(2)}) copy-start(f32[2,144,768]{2,1,0:T(8,128)} %get-tuple-element.21) | copy-start | bytes 2654212
  282.8 1.0 copy-start.3
  283.8 1.2 copy-start.1
  285.0 1.2 copy-start.2

commit v4 on v3

--- a/solution.py
+++ b/solution.py
@@ -549,7 +549,7 @@
     def dd_of(i):
         return lax.rem(d + i, n_dp)
 
-    def rdma(src, dst, rsem, to_d, to_c):
+    def rdma(src, dst, rsem, to_d, to_c, when=None):
         ssem = s_send.at[counter[0]]
         counter[0] += 1
         copy = pltpu.make_async_remote_copy(
@@ -560,9 +560,19 @@
             device_id=(to_d, to_c),
             device_id_type=MESH,
         )
-        copy.start()
-        pending.append(copy)
-        return copy
+        if when is None:
+            copy.start()
+        else:
+            pl.when(when)(copy.start)
+        pending.append((copy, when))
+        return pending[-1]
+
+    def sent(entry):
+        copy, when = entry
+        if when is None:
+            copy.wait_send()
+        else:
+            pl.when(when)(copy.wait_send)
 
     def arrived(dst, rsem):
         pltpu.make_async_remote_copy(
@@ -574,12 +584,66 @@
             device_id_type=MESH,
         ).wait_recv()
 
+    middle = (z == 1) | (z == 2)
+    hop = {1: z != n_z - 1, 2: None, 3: z != 0}
+
+    def z_spread(ref, sem):
+        return [
+            rdma(ref(z), ref(z), sem(n_z - i), d, zc(i), when=hop[i]) for i in (2, 1, 3)
+        ]
+
+    def z_relay(ref, sem):
+        e = lax.rem(z + 2, n_z)
+        to = lax.rem(3 * (z + 3), n_z)
+        arrived(ref(e), sem(2))
+        return rdma(
+            ref(e), ref(e), sem(lax.rem(e + n_z - to, n_z)), d, 2 * to + k, when=middle
+        )
+
+    def z_reduce(part, slot, sem):
+        edge = (z == 0) | (z == n_z - 1)
+        to = 1 + z // 3
+        rdma(part(n_z - 1 - z), slot(n_z - 1), sem(n_z - 1), d, 2 * to + k, when=edge)
+        for i in (1, 3):
+            there = n_z - i - 1
+            rdma(
+                part(lax.rem(z + i, n_z)), slot(there), sem(there), d, zc(i), when=hop[i]
+            )
+
+    def z_reduce_rest(part, slot, sem):
+        far = part(lax.rem(z + 2, n_z))
+
+        @pl.when(middle)
+        def _():
+            arrived(slot(n_z - 1), sem(n_z - 1))
+            far[...] = (far[...].astype(F32) + slot(n_z - 1)[...].astype(F32)).astype(BF)
+
+        rdma(far, slot(1), sem(1), d, zc(2))
+
+    def z_collect(total, slot, sem):
+        arrived(slot(1), sem(1))
+        total[...] += slot(1)[...].astype(F32)
+        for j, there in ((0, z != n_z - 1), (2, z != 0)):
+
+            @pl.when(there)
+            def _():
+                arrived(slot(j), sem(j))
+                total[...] += slot(j)[...].astype(F32)
+
+    def wa(e):
+        return wt.at[d, e, k, :, la]
+
+    def wb(e):
+        return wt.at[d, e, k, :, lb]
+
+    def row_half(e):
+        return (lambda j: big.at[k, e, j]), (lambda j: s_gu.at[e, j])
+
     wt[d, z, k] = w_pack[...]
     gb[c] = gains[...]
     la = pl.ds(0, 512)
     lb = pl.ds(512, pack - 512)
-    for i in range(1, n_z):
-        rdma(wt.at[d, z, k, :, la], wt.at[d, z, k, :, la], s_a.at[0, n_z - i], d, zc(i))
+    z_spread(wa, lambda j: s_a.at[0, j])
     for i in range(1, n_dp):
         rdma(wt.at[d, z, k, :, la], wt.at[d, z, k, :, la], s_a.at[n_dp - i, 0], dd_of(i), c)
     for i in range(1, n_ctx):
@@ -593,27 +657,24 @@
     def down_rows(e):
         return pl.ds(pl.multiple_of(e * cq, 32), cq)
 
-    def spread_rows(e):
-        for i in range(1, n_z):
-            copy = rdma(big.at[k, e, z], big.at[k, e, z], s_gu.at[e, n_z - i], d, zc(i))
-            big_sends.append(copy)
-
-    for i in range(1, n_z):
-        rdma(wt.at[d, z, k, :, lb], wt.at[d, z, k, :, lb], s_bz.at[n_z - i], d, zc(i))
-    for i in range(1, n_z):
-        rdma(wdz.at[z], wdz.at[z], s_wdz.at[n_z - i], d, zc(i))
-    spread_rows(0)
+    z_spread(wb, lambda j: s_bz.at[j])
+    z_spread(lambda j: wdz.at[j], lambda j: s_wdz.at[j])
+    big_sends.extend(z_spread(*row_half(0)))
     stream = tok[...].astype(F32)
     inv1 = lax.rsqrt(jnp.mean(stream * stream, axis=1, keepdims=True) + norm_eps)
 
-    for q in (1, n_z - 1, 2):
+    z_relay(wa, lambda j: s_a.at[0, j])
+    for q in (2, 1, 3):
         zq = lax.rem(z + q, n_z)
-        arrived(wt.at[d, zq, k, :, la], s_a.at[0, q])
+        if q != 2:
+            arrived(wt.at[d, zq, k, :, la], s_a.at[0, q])
         for i in range(1, n_dp):
             rdma(
                 wt.at[d, zq, k, :, la], wt.at[d, zq, k, :, la], s_a.at[n_dp - i, q], dd_of(i), c
             )
     rdma(wt.at[d, :, k, :, la], wt.at[d, :, k, :, la], s_ap.at[0], d, mate)
+    z_relay(wb, lambda j: s_bz.at[j])
+    z_relay(lambda j: wdz.at[j], lambda j: s_wdz.at[j])
     for r in range(1, n_dp):
         dr = dd_of(r)
         for q in range(n_z):
@@ -644,6 +705,7 @@
         kt[pl.ds(pl.multiple_of(model // 3 + e * ck, 32), ck), :] = o_t[cq + ck : cq + 2 * ck]
         return 0
 
+    big_sends.append(z_relay(*row_half(0)))
     lax.fori_loop(0, n_dp, project, 0)
     cosine = cos_ref[...]
     sine = sin_ref[...]
@@ -660,22 +722,24 @@
         lo, hi = turn(kt[g * hs : g * hs + half], kt[g * hs + half : (g + 1) * hs])
         kvb[c, 128 * g : 128 * g + 64, :] = jnp.concatenate([lo, hi], axis=0).astype(BF)
         kvb[c, 128 * g + 64 : 128 * g + 128, :] = kt[kvw + g * hs : kvw + (g + 1) * hs].astype(BF)
-    for i in range(1, n_z):
-        rdma(kvb.at[c], kvb.at[c], s_kv.at[n_z - i], d, zc(i))
+    def kv_of(j):
+        return kvb.at[2 * j + k]
+
+    z_spread(kv_of, lambda j: s_kv.at[j])
     rdma(kvb.at[c], kvb.at[c], s_kv.at[n_z], d, mate)
-    spread_rows(1)
+    big_sends.extend(z_spread(*row_half(1)))
     for h in range(kvh * group):
         lo, hi = turn(at[h * hs : h * hs + half], at[h * hs + half : (h + 1) * hs])
         low = jnp.concatenate([lo, hi], axis=0).astype(BF)
         qt[h * hs : (h + 1) * hs, :] = (low.astype(F32) * 0.125).astype(BF)
 
-    for q in range(1, n_z):
+    for q in (1, 3):
         zq = lax.rem(z + q, n_z)
         arrived(wt.at[d, zq, k, :, lb], s_bz.at[q])
     for i in range(1, n_dp):
         rdma(wt.at[d, :, k, :, lb], wt.at[d, :, k, :, lb], s_b.at[n_dp - i], dd_of(i), c)
     rdma(wt.at[d, :, k, :, lb], wt.at[d, :, k, :, lb], s_bp.at[0], d, mate)
-    for q in range(1, n_z):
+    for q in (1, 3):
         arrived(wdz.at[lax.rem(z + q, n_z)], s_wdz.at[q])
     for i in range(1, n_dp):
         e = dd_of(i)
@@ -683,8 +747,10 @@
     wd[down_rows(d), pl.ds(my_down, rf)] = wdz[d]
     for i in range(1, n_dp):
         rdma(cb.at[own], cb.at[n_dp - i - 1], s_c.at[n_dp - i - 1], dd_of(i), c)
-    for q in range(1, n_z):
-        arrived(kvb.at[zc(q)], s_kv.at[q])
+    z_relay(kv_of, lambda j: s_kv.at[j])
+    for q in (2, 1, 3):
+        if q != 2:
+            arrived(kvb.at[zc(q)], s_kv.at[q])
         rdma(kvb.at[zc(q)], kvb.at[zc(q)], s_kv.at[n_z + q], d, mate)
     for r in range(1, n_dp):
         dr = dd_of(r)
@@ -743,12 +809,14 @@
     for r in range(1, n_dp):
         arrived(wd.at[down_rows(dd_of(r)), pl.ds(my_down, rf)], s_wd.at[r])
     rdma(wd.at[:, pl.ds(my_down, rf)], wd.at[:, pl.ds(my_down, rf)], s_wd.at[0], d, mate)
+    big_sends.append(z_relay(*row_half(1)))
     for e in range(2):
         copy = rdma(big.at[k, e, z], big.at[k, e, z], s_gu.at[e, n_z], d, mate)
         big_sends.append(copy)
-        for q in range(1, n_z):
+        for q in (2, 1, 3):
             zq = lax.rem(z + q, n_z)
-            arrived(big.at[k, e, zq], s_gu.at[e, q])
+            if q != 2:
+                arrived(big.at[k, e, zq], s_gu.at[e, q])
             copy = rdma(big.at[k, e, zq], big.at[k, e, zq], s_gu.at[e, n_z + q], d, mate)
             big_sends.append(copy)
 
@@ -899,11 +967,8 @@
         return 0
 
     lax.fori_loop(0, 2 * n_z, gu_sum, 0)
-    for i in range(1, n_z):
-        there = n_z - i - 1
-        rdma(
-            gu_r.at[:, lax.rem(z + i, n_z)], gu_z.at[there], s_gur.at[there + 1], d, zc(i)
-        )
+    gu_set = (lambda j: gu_r.at[:, j], lambda j: gu_z.at[j], lambda j: s_gur.at[j + 1])
+    z_reduce(*gu_set)
     arrived(gd_r, s_gdr.at[0])
 
     def gd_sum(e, _):
@@ -916,7 +981,7 @@
     gd_p[d] = gd_r[d]
 
     for copy in big_sends:
-        copy.wait_send()
+        sent(copy)
     pending[:] = [copy for copy in pending if all(copy is not other for other in big_sends)]
 
     def store_pack(e, n0, t):
@@ -949,25 +1014,24 @@
             t = t + g_p[p, j, :, lanes].astype(F32)
         return t
 
+    def pack_set(s, lanes):
+        return (
+            lambda j: g_r.at[d, j, :, lanes],
+            lambda j: g_z.at[j, :, lanes],
+            lambda j: s_gz.at[s, j],
+        )
+
     def to_z(s, lanes):
         for p in range(n_dp - 1):
             arrived(g_p.at[p, :, :, lanes], s_gp.at[s, p])
         for i in range(1, n_z):
             zq = lax.rem(z + i, n_z)
-            there = n_z - i - 1
             g_r[d, zq, :, lanes] = plane_sum(zq, lanes).astype(BF)
-            rdma(
-                g_r.at[d, zq, :, lanes], g_z.at[there, :, lanes], s_gz.at[s, there], d, zc(i)
-            )
+        z_reduce(*pack_set(s, lanes))
         g_pack_ref[:, lanes] = plane_sum(z, lanes)
 
     def last_sum(s, lanes):
-        for i in range(n_z - 1):
-            arrived(g_z.at[i, :, lanes], s_gz.at[s, i])
-        t = g_pack_ref[:, lanes]
-        for i in range(n_z - 1):
-            t = t + g_z[i, :, lanes].astype(F32)
-        g_pack_ref[:, lanes] = t
+        z_collect(g_pack_ref.at[:, lanes], *pack_set(s, lanes)[1:])
 
     for r in (1, 2, 3, 0):
         e = dd_of(r)
@@ -977,6 +1041,7 @@
         store_pack(e, 512, t)
         rdma(big.at[1 - k, e, :, :, lb], g_r.at[e, :, :, lb], s_gr.at[1, r], d, mate)
     to_plane(1, lb)
+    z_reduce_rest(*gu_set)
 
     def attend_back(g, _):
         q_t = heads_of(qt, g)
@@ -1018,16 +1083,15 @@
         return 0
 
     lax.fori_loop(0, n_z, kv_sum, 0)
-    for i in range(1, n_z):
-        there = n_z - i - 1
-        rdma(dkv_r.at[lax.rem(z + i, n_z)], dkv_z.at[there], s_dkv.at[there + 1], d, zc(i))
+    kv_set = (lambda j: dkv_r.at[j], lambda j: dkv_z.at[j], lambda j: s_dkv.at[j + 1])
+    z_reduce(*kv_set)
+    z_reduce_rest(*kv_set)
     chip_sum(0, 1, lb)
     to_z(1, lb)
     for r in range(1, n_dp):
         arrived(gd_p.at[dd_of(r)], s_gdp.at[r])
-    for i in range(1, n_z):
-        there = n_z - i - 1
-        rdma(gd_p.at[lax.rem(z + i, n_z)], gd_z.at[there], s_gdz.at[there], d, zc(i))
+    gd_set = (lambda j: gd_p.at[j], lambda j: gd_z.at[j], lambda j: s_gdz.at[j])
+    z_reduce(*gd_set)
 
     for p in range(n_dp - 1):
         arrived(orecv.at[p], s_o.at[p])
@@ -1036,12 +1100,9 @@
         y_all = y_all + orecv[p].astype(F32)
     out_ref[...] = y_all.astype(BF)
 
-    for i in range(n_z - 1):
-        arrived(dkv_z.at[i], s_dkv.at[i + 1])
-    kv_total = dkv_r[z].astype(F32)
-    for i in range(n_z - 1):
-        kv_total = kv_total + dkv_z[i].astype(F32)
-    kvsum[...] = kv_total
+    kvsum[...] = dkv_r[z].astype(F32)
+    z_collect(kvsum, *kv_set[1:])
+    z_reduce_rest(*pack_set(1, lb))
     for g in range(kvh):
         r = 128 * g
         lo, hi = turn_back(kvsum[r : r + half], kvsum[r + half : r + hs])
@@ -1070,6 +1131,7 @@
         lax.fori_loop(0, 512 // nc, pack_cols, 0)
         rdma(big.at[1 - k, e, :, :, la], g_r.at[e, :, :, la], s_gr.at[0, r], d, mate)
 
+    z_reduce_rest(*gd_set)
     to_plane(0, la)
 
     dna[...] = jnp.zeros_like(dna)
@@ -1096,21 +1158,13 @@
     gg_c[0] = gg_all
     for i in range(1, n_ctx):
         rdma(gg_c.at[0], gg_c.at[n_ctx - i], s_ggc.at[n_ctx - i], d, lax.rem(c + i, n_ctx))
-    for i in range(n_z - 1):
-        arrived(gu_z.at[i], s_gur.at[i + 1])
-    for e in range(2):
-        t = gu_r[e, z].astype(F32)
-        for i in range(n_z - 1):
-            t = t + gu_z[i, e].astype(F32)
-        g_gu_ref[e] = t
-    for i in range(n_z - 1):
-        arrived(gd_z.at[i], s_gdz.at[i])
-    t = gd_p[z].astype(F32)
-    for i in range(n_z - 1):
-        t = t + gd_z[i].astype(F32)
-    g_down_ref[...] = t
+    g_gu_ref[...] = gu_r[:, z].astype(F32)
+    z_collect(g_gu_ref, *gu_set[1:])
+    g_down_ref[...] = gd_p[z].astype(F32)
+    z_collect(g_down_ref, *gd_set[1:])
     last_sum(1, lb)
     to_z(0, la)
+    z_reduce_rest(*pack_set(0, la))
     for i in range(1, n_ctx):
         arrived(gg_c.at[i], s_ggc.at[i])
     gg_tot = gg_c[0]
@@ -1119,7 +1173,7 @@
     gg_ref[...] = shift_lanes(gg_tot, lax.rem(model - shard_rows * c, model))[:, :256]
     last_sum(0, la)
     for copy in pending:
-        copy.wait_send()
+        sent(copy)
 def fast_body(
     n_dp,
     n_ctx,
@@ -1158,7 +1212,6 @@
     vm = pl.BlockSpec(memory_space=pltpu.VMEM)
     dma = pltpu.SemaphoreType.DMA
     n = n_dp - 1
-    m = n_z - 1
     scratch = [
         pltpu.VMEM((n_ctx, 8, 256), F32),
         pltpu.VMEM((n_dp, n_z, 2, sr, pack), BF),
@@ -1189,22 +1242,22 @@
         pltpu.VMEM((n_dp, 2 * rows_tok, pack), BF),
         pltpu.VMEM((2, n_z, 2 * model // 3, rows_tok), BF),
         pltpu.VMEM((n_z, 2 * model // 3, rows_tok), BF),
-        pltpu.VMEM((m, 2 * model // 3, rows_tok), BF),
+        pltpu.VMEM((n_z, 2 * model // 3, rows_tok), BF),
         pltpu.VMEM((2 * model // 3, rows_tok), F32),
         pltpu.VMEM((2, n_z, sr, ffs), BF),
-        pltpu.VMEM((m, 2, sr, ffs), BF),
+        pltpu.VMEM((n_z, 2, sr, ffs), BF),
         pltpu.VMEM((2, n_dp, cd, rf), BF),
         pltpu.VMEM((n_dp, cd, rf), BF),
         pltpu.VMEM((n_dp, cd, rf), BF),
-        pltpu.VMEM((m, cd, rf), BF),
+        pltpu.VMEM((n_z, cd, rf), BF),
         pltpu.VMEM((n_dp, n_z, sr, pack), BF),
         pltpu.VMEM((n, n_z, sr, pack), BF),
-        pltpu.VMEM((m, sr, pack), BF),
+        pltpu.VMEM((n_z, sr, pack), BF),
         pltpu.VMEM((model, 2 * rows_tok), BF),
         pltpu.VMEM((8, model), F32),
         pltpu.VMEM((n, 8, model), F32),
         pltpu.VMEM((n_ctx, 8, model), F32),
-        dma((150,)),
+        dma((170,)),
         dma((n_ctx,)),
         dma((n_dp, n_z)),
         dma((n_dp,)),
@@ -1219,14 +1272,14 @@
         dma((n,)),
         dma((n,)),
         dma((n,)),
-        dma((n_z,)),
-        dma((n_z,)),
+        dma((n_z + 1,)),
+        dma((n_z + 1,)),
         dma((1,)),
         dma((n_dp,)),
-        dma((m,)),
+        dma((n_z,)),
         dma((2, n_dp)),
         dma((2, n)),
-        dma((2, m)),
+        dma((2, n_z)),
         dma((n,)),
         dma((n_ctx,)),
     ]

time: 288 us -> 250 us (0.87)
  Pallas kernels: 273 us -> 236 us
    pallas_call x1, Pallas kernels: 273 us -> 236 us  [fast_body(): pl.pallas_call(functools.partial(fast_kernel, n_dp, n_ctx), out_shape=(ja...]
where the time goes in v4:
time: 250 us
  Pallas kernels  236 us (94%)
  local copies, waits for them, and re-layouts  10.3 us (4%)
  other arithmetic  3.15 us (1%)
    pallas_call x1, Pallas kernels, fast_body(): pl.pallas_call(functools.partial(fast_kernel, n_dp, n_ctx), out_shape=(ja...  236 us

profile of v4, /device:TPU:0, one launch (start us, length us, event | category | flops | bytes accessed | tf_op | source)
XLA Modules:
  0.0 249.7 jit_solution(4134079483671084619)
XLA Ops:
  0.6 0.0 copy-start.4
  0.7 0.7 stack.9
  1.3 0.7 stack.10
  2.0 0.6 fusion.6.gains
  2.6 0.8 multiply_sine_fusion
  3.4 0.0 copy-done.4
  3.4 1.8 pad_maximum_fusion.w_pack
  5.1 235.5 %layer.1 = (bf16[128,1152]{1,0:T(8,128)(2,1)}, f32[128,1152]{1,0:T(8,128)}, f32[8,256]{1,0:T(8,128)}, f32[144,768]{1,0:T(8,128)}, f32[2,144,768]{2,1,0:T(8,128)}, /*index=5*/f32[288,384]{1,0:T(8,128)}) custom-call(bf16[128,1152]{1,0:T(8,128)(2,1)} %bitcast.15, bf16[128,1152]{1,0:T(8,128)(2,1)} %bitcast.16, s32[1,4]{1,0:T(1,128)} %starts.1, ...), custom_call_target="tpu_custom_call" | custom-call | tf_op jit(solution)/shard_map/layer/pallas_call | solution.py:1286
  240.7 0.0 copy-start
  240.7 1.4 fusion.9
  242.0 1.6 fusion.8
  243.7 1.9 fusion.7
  245.5 0.0 copy-done
  245.5 0.0 copy-start.3
  245.5 1.0 slice_bitcast_fusion
  246.5 0.0 copy-start.1
  246.5 0.0 copy-done.3
  246.5 0.7 copy.26
  247.2 0.4 copy-done.1
  247.7 0.0 copy-start.2
  247.7 0.8 copy.27
  248.5 0.4 copy-done.2
  248.9 0.8 copy.28
  (2 shorter events, 0.0 us)
Async XLA Ops:
  0.6 2.7 %copy-start.4 = (bf16[144,96]{1,0:T(8,128)(2,1)S(1)}, bf16[144,96]{1,0:T(8,128)(2,1)}, u32[]{:S(2)}) copy-start(bf16[144,96]{1,0:T(8,128)(2,1)} %param.18) | copy-start | bytes 82948
  240.7 4.9 %copy-start = (f32[2,144,768]{2,1,0:T(8,128)S(1)}, f32[2,144,768]{2,1,0:T(8,128)}, u32[]{:S(2)}) copy-start(f32[2,144,768]{2,1,0:T(8,128)} %get-tuple-element.21) | copy-start | bytes 2654212
  245.5 1.0 copy-start.3
  246.5 1.2 copy-start.1
  247.7 1.2 copy-start.2
